TPU v7x, 32 devices: a whole 2x2x4 slice. The times are simulated.
32 devices in a mesh: dp: 2 (over y), fsdp: 16 (over z, x, core).
Axes of the slice: x: 2, y: 2, z: 4, core: 2. Of those that a mesh axis runs over, the one named last changes fastest.
Arguments:
- ids: int32 [2, 192], P('dp'), may hold values from 0 to 511
- embed: bfloat16 [512, 8192], P(None, 'fsdp'), may hold values from -32 to 32
- gain: bfloat16 [8192], P('fsdp'), may hold values from 0.099609375 to 1.8984375
- w_in: bfloat16 [3, 4096, 8192], P(None, 'fsdp'), may hold values from -0.0625 to 0.0625
- feat_filter: float32 [3, 256, 7], P(None, 'fsdp'), may hold values from -2.4 to 2.4
- inner_filter: float32 [256, 7], P('fsdp'), may hold values from -2.4 to 2.4
- w_out: bfloat16 [4096, 8192], P(None, 'fsdp'), may hold values from -0.09375 to 0.09375
- cotangent: bfloat16 [2, 192, 8192], P('dp', None, 'fsdp'), may hold values from -6 to 6
- right_prev: bfloat16 [8192, 256], P('fsdp'), may hold values from -6 to 6
Outputs:
- block_out: bfloat16 [2, 192, 8192], P('dp', None, 'fsdp')
- filter_grad: float32 [4, 256, 7], P(None, 'fsdp')
- basis: bfloat16 [4096, 256], P('fsdp')
- right_factor: float32 [8192, 256], P('fsdp')
All inputs are finite; a program needn't handle non-finite values.
Results may differ from a plain program's by a relative error of at most 0.014.
The roundings to bfloat16 on the way count: a program that leaves them out, or rounds other values in their place, can miss the bound.
Values may be sent and summed in bfloat16 or wider, within the bound.
No kernel may reach another device: no remote copies, remote signals or barrier semaphores. Data moves between devices by JAX's collectives and lax.ppermute only.
A program may use at most 128 MiB of HBM per device.

v0:
```python
import jax
import jax.numpy as jnp
from jax import lax
from jax.sharding import PartitionSpec as P

D = 8192
C = 4096
GROUP = 16


def shifted(signal, lag, tap_count):
    padded = jnp.pad(signal, ((tap_count - 1, 0), (0, 0)))
    first = tap_count - 1 - lag
    return padded[first : first + signal.shape[0]]


def causal(signal, tap_table):
    tap_count = tap_table.shape[0]
    result = jnp.zeros(signal.shape, jnp.float32)
    for lag in range(tap_count):
        result = result + tap_table[lag][None, :] * shifted(signal, lag, tap_count)
    return result


def anticausal(signal, tap_table):
    tap_count = tap_table.shape[0]
    padded = jnp.pad(signal, ((0, tap_count - 1), (0, 0)))
    result = jnp.zeros(signal.shape, jnp.float32)
    for lag in range(tap_count):
        result = result + tap_table[lag][None, :] * padded[lag : lag + signal.shape[0]]
    return result


def tap_sums(gradient, signal, tap_count):
    listing = []
    for lag in range(tap_count):
        listing.append(jnp.sum(gradient * shifted(signal, lag, tap_count), axis=0))
    stacked = jnp.stack(listing, axis=0)
    grouped = stacked.reshape(tap_count, stacked.shape[1] // GROUP, GROUP).sum(axis=2)
    return grouped.T


def expand(filters):
    return jnp.repeat(filters.T, GROUP, axis=1)


def per_device(ids, embed, gain, w_in, feat_filter, inner_filter, w_out, cotangent, right_prev):
    tokens = ids[0]
    length = tokens.shape[0]
    tap_count = inner_filter.shape[1]
    onehot = (tokens[:, None] == jnp.arange(embed.shape[0], dtype=jnp.int32)[None, :]).astype(
        jnp.bfloat16
    )
    x_cols = jnp.dot(onehot, embed, preferred_element_type=jnp.float32)
    square_sums = lax.psum(jnp.sum(x_cols * x_cols, axis=1), "fsdp")
    factor = lax.rsqrt(square_sums / D + 1e-05)
    normed_cols = (x_cols * factor[:, None] * gain.astype(jnp.float32)[None, :]).astype(
        jnp.bfloat16
    )
    projected = jnp.einsum(
        "ld,kcd->klc",
        lax.all_gather(normed_cols, "fsdp", axis=1, tiled=True),
        w_in,
        preferred_element_type=jnp.float32,
    )
    rounded = lax.optimization_barrier(projected.astype(jnp.bfloat16)).astype(jnp.float32)
    query, key_in, value = (rounded[0], rounded[1], rounded[2])
    query_conv = causal(query, expand(feat_filter[0]))
    key_conv = causal(key_in, expand(feat_filter[1]))
    value_conv = causal(value, expand(feat_filter[2]))
    gated = key_conv * value_conv
    inner_table = expand(inner_filter)
    window = causal(gated, inner_table)
    gated_out = (query_conv * window).astype(jnp.bfloat16)
    cot_cols = cotangent[0]
    shard_piece = lax.all_gather(gated_out, "fsdp", axis=1, tiled=True)
    weight_rows = w_out
    mixed_sum = jnp.dot(shard_piece, weight_rows, preferred_element_type=jnp.float32)
    term = jnp.einsum("lc,ld->cd", shard_piece, cot_cols, preferred_element_type=jnp.float32)
    mixed_sum, grad_part = (mixed_sum, term)
    block_out = (x_cols + mixed_sum).astype(jnp.bfloat16)[None]
    weight_rows = w_out
    mixed_grad = lax.psum_scatter(
        jnp.einsum("cd,ld->cl", weight_rows, cot_cols, preferred_element_type=jnp.float32),
        "fsdp",
        scatter_dimension=0,
        tiled=True,
    ).T
    query_grad = mixed_grad * window
    window_grad = mixed_grad * query_conv
    gated_grad = anticausal(window_grad, inner_table)
    key_grad = gated_grad * value_conv
    value_grad = gated_grad * key_conv
    norm_factor = 1.0 / jnp.sqrt(jnp.float32(lax.axis_size("dp") * length))
    filter_part = (
        jnp.stack(
            [
                tap_sums(query_grad, query, tap_count),
                tap_sums(key_grad, key_in, tap_count),
                tap_sums(value_grad, value, tap_count),
                tap_sums(window_grad, gated, tap_count),
            ],
            axis=0,
        )
        * norm_factor
    )
    grad_total, filter_grad = (
        lax.psum(grad_part.astype(jnp.bfloat16), "dp").astype(jnp.float32),
        lax.psum(filter_part.astype(jnp.bfloat16), "dp").astype(jnp.float32),
    )
    grad_half = grad_total.astype(jnp.bfloat16)
    grad_rows_own = lax.all_to_all(grad_half, "fsdp", split_axis=0, concat_axis=1, tiled=True)
    panel_own = jnp.dot(
        grad_rows_own,
        lax.all_gather(right_prev, "fsdp", axis=0, tiled=True),
        preferred_element_type=jnp.float32,
    ).astype(jnp.bfloat16)
    root_scale = jnp.sqrt(jnp.float32(C))
    gram_local = jnp.einsum("cr,cs->rs", panel_own, panel_own, preferred_element_type=jnp.float32)
    gram_matrix = lax.psum(gram_local, "fsdp")
    lower_factor = jnp.linalg.cholesky(gram_matrix)
    solved = jax.scipy.linalg.solve_triangular(
        lower_factor, panel_own.astype(jnp.float32).T, lower=True
    ).T
    basis_own = (solved * root_scale).astype(jnp.bfloat16)
    right_raw = jnp.einsum(
        "cd,cr->dr",
        grad_half,
        lax.all_gather(basis_own, "fsdp", axis=0, tiled=True),
        preferred_element_type=jnp.float32,
    )
    column_sums = lax.psum(jnp.sum(right_raw * right_raw, axis=0), "fsdp")
    right_factor = right_raw * lax.rsqrt(column_sums / D + 1e-06)[None, :]
    return (block_out, filter_grad, basis_own, right_factor)


def solution(mesh):
    placed = (
        P("dp", None),
        P(None, "fsdp"),
        P("fsdp"),
        P(None, "fsdp", None),
        P(None, "fsdp", None),
        P("fsdp", None),
        P(None, "fsdp"),
        P("dp", None, "fsdp"),
        P("fsdp", None),
    )
    return jax.shard_map(
        per_device,
        mesh=mesh,
        in_specs=placed,
        out_specs=(P("dp", None, "fsdp"), P(None, "fsdp", None), P("fsdp", None), P("fsdp", None)),
        check_vma=False,
    )
```

profile of v0, /device:TPU:0, one launch (start us, length us, event | category | flops | bytes accessed | tf_op | source)
XLA Modules:
  0.0 699.4 jit_solution(17935779332028869934)
XLA Ops:
  9.3 34.9 %psum.35 = f32[192]{0:T(256)S(1)} all-reduce(f32[192]{0:T(256)S(1)} %get-tuple-element.121), channel_id=1, replica_groups=mesh['dp'=2,'fsdp'=16] {'fsdp'}, use_global_device_ids=true, to_apply=%region_1.0 | all-reduce | flops 192 | bytes 1536 | tf_op jit(solution)/shard_map/psum | solution.py:55
  45.1 5.4 fusion.14
  55.0 34.7 %all-gather.5.cloned.1.call-done = bf16[192,8192]{1,0:T(8,128)(2,1)} async-done(((bf16[192,512]{1,0:T(8,128)(2,1)}), bf16[192,8192]{1,0:T(8,128)(2,1)}) %all-gather.5.cloned.1.call-update) | async-done | bytes 3145744 | tf_op jit(solution)/shard_map/all_gather | solution.py:62
  89.7 9.8 %fusion.6 = bf16[3,192,256]{2,1,0:T(8,128)(2,1)S(1)} fusion(bf16[3,256,8192]{2,1,0:T(8,128)(2,1)} %param.12, bf16[192,8192]{1,0:T(8,128)(2,1)} %all-gather.5.cloned.1.call-done), kind=kOutput, calls=%fused_computation.8 | convolution fusion | flops 2416066560 | bytes 16023552 | tf_op jit(solution)/shard_map/ld,kcd->klc/dot_general | solution.py:60
  99.6 58.3 %reduce-scatter.2.cloned.1.call-done = f32[256,192]{0,1:T(8,128)} async-done(((f32[4096,192]{0,1:T(8,128)}), f32[256,192]{0,1:T(8,128)}) %reduce-scatter.2.cloned.1.call-update) | async-done | bytes 196624 | tf_op jit(solution)/shard_map/reduce_scatter | solution.py:83
  164.3 38.0 %all-gather.7.cloned.1.call-done = bf16[192,4096]{1,0:T(8,128)(2,1)} async-done(((bf16[192,256]{1,0:T(8,128)(2,1)}), bf16[192,4096]{1,0:T(8,128)(2,1)}) %all-gather.7.cloned.1.call-update) | async-done | bytes 1572880 | tf_op jit(solution)/shard_map/all_gather | solution.py:76
  202.3 4.7 convolution_convert_fusion
  207.7 106.5 %all-reduce.9.cloned.1.call-done = bf16[4096,512]{1,0:T(8,128)(2,1)} async-done(((bf16[4096,512]{1,0:T(8,128)(2,1)}), bf16[4096,512]{1,0:T(8,128)(2,1)}) %all-reduce.9.cloned.1.call-update) | async-done | bytes 4194320 | tf_op jit(solution)/shard_map/psum | solution.py:108
  314.2 6.4 copy.22
  320.6 5.7 all-to-all-start
  326.3 94.7 %all-gather.9.cloned.1.call-done = bf16[8192,256]{1,0:T(8,128)(2,1)} async-done(((bf16[512,256]{1,0:T(8,128)(2,1)}), bf16[8192,256]{1,0:T(8,128)(2,1)}) %all-gather.9.cloned.1.call-update) | async-done | bytes 4194320 | tf_op jit(solution)/shard_map/all_gather | solution.py:115
  421.0 6.5 all-to-all-done
  427.4 4.8 convolution_convert_fusion.1
  434.0 103.0 %all-reduce.11.cloned.1.call-done = f32[256,256]{0,1:T(8,128)} async-done(((f32[256,256]{0,1:T(8,128)}), f32[256,256]{0,1:T(8,128)}) %all-reduce.11.cloned.1.call-update) | async-done | bytes 262160 | tf_op jit(solution)/shard_map/psum | solution.py:120
  540.6 11.7 %cholesky.50 = f32[128,128]{1,0:T(8,128)S(1)} custom-call(f32[128,128]{1,0:T(8,128)S(1)} %cholesky.118), custom_call_target="Cholesky" | custom-call | tf_op jit(solution)/shard_map/jit(cholesky)/cholesky | solution.py:121
  553.6 9.8 %custom-call.15 = f32[1,128,128]{1,2,0:T(8,128)S(1)} custom-call(f32[1,128,128]{2,1,0:T(8,128)S(1)} %get-tuple-element.89), custom_call_target="InvertDiagBlocksLowerTriangular" | custom-call | tf_op jit(solution)/shard_map/jit(cholesky)/cholesky | solution.py:121
  566.2 11.7 %cholesky.105 = f32[128,128]{1,0:T(8,128)S(1)} custom-call(f32[128,128]{1,0:T(8,128)S(1)} %convolution_subtract_fusion.1), custom_call_target="Cholesky" | custom-call | tf_op jit(solution)/shard_map/jit(cholesky)/cholesky | solution.py:121
  584.2 6.8 while.1
  591.0 20.5 %custom-call.16 = f32[2,128,128]{1,2,0:T(8,128)S(1)} custom-call(f32[2,128,128]{2,1,0:T(8,128)} %get-tuple-element.11), custom_call_target="InvertDiagBlocksLowerTriangular" | custom-call | tf_op jit(solution)/shard_map/jit(_solve_triangular)/triangular_solve | solution.py:122
  622.1 5.0 psum.36
  627.8 3.8 fusion.9
  632.4 23.5 %all-gather.11.cloned.1.call-done = bf16[4096,256]{0,1:T(8,128)(2,1)} async-done(((bf16[256,256]{0,1:T(8,128)(2,1)}), bf16[4096,256]{0,1:T(8,128)(2,1)}) %all-gather.11.cloned.1.call-update) | async-done | bytes 2097168 | tf_op jit(solution)/shard_map/all_gather | solution.py:129
  655.9 4.2 multiply_reduce_fusion
  660.1 31.6 %psum.39 = f32[256]{0:T(256)S(1)} all-reduce(f32[256]{0:T(256)S(1)} %get-tuple-element.125), channel_id=1, replica_groups=mesh['dp'=2,'fsdp'=16] {'fsdp'}, use_global_device_ids=true, to_apply=%region_43.44 | all-reduce | flops 256 | bytes 2048 | tf_op jit(solution)/shard_map/psum | solution.py:132
  (198 shorter events, 48.3 us)
Async XLA Ops:
  7.2 1.1 copy-start
  7.2 82.5 %all-gather.5.cloned.1.call-start = ((), (), s32[]{:S(2)}) async-start(), calls=%async_computation.2 | async-start | bytes 3342336 | tf_op jit(solution)/shard_map/all_gather | solution.py:62
  45.0 5.5 copy-start.8
  45.0 6.6 copy-start.9
  45.1 112.9 %reduce-scatter.2.cloned.1.call-start = ((), (), s32[]{:S(2)}) async-start(), calls=%async_computation.4 | async-start | bytes 3342336 | tf_op jit(solution)/shard_map/reduce_scatter | solution.py:83
  50.5 151.8 %all-gather.7.cloned.1.call-start = ((), (), s32[]{:S(2)}) async-start(), calls=%async_computation.3 | async-start | bytes 1671168 | tf_op jit(solution)/shard_map/all_gather | solution.py:76
  99.5 102.8 %copy-start.7 = (bf16[1,192,512]{2,1,0:T(8,128)(2,1)S(1)}, bf16[1,192,512]{2,1,0:T(8,128)(2,1)}, u32[]{:S(2)}) copy-start(bf16[1,192,512]{2,1,0:T(8,128)(2,1)} %param.16) | copy-start | bytes 589828
  99.6 61.3 %copy-start.3 = (f32[192,256]{1,0:T(8,128)}, f32[192,256]{1,0:T(8,128)S(1)}, u32[]{:S(2)}) copy-start(f32[192,256]{1,0:T(8,128)S(1)} %get-tuple-element.84) | copy-start | bytes 589828
  159.1 48.0 %copy-start.4 = (f32[192,256]{1,0:T(8,128)}, f32[192,256]{1,0:T(8,128)S(1)}, u32[]{:S(2)}) copy-start(f32[192,256]{1,0:T(8,128)S(1)} %get-tuple-element.79) | copy-start | bytes 589828
  161.0 46.1 %copy-start.2 = (f32[192,256]{1,0:T(8,128)}, f32[192,256]{1,0:T(8,128)S(1)}, u32[]{:S(2)}) copy-start(f32[192,256]{1,0:T(8,128)S(1)} %mul.459) | copy-start | bytes 589828
  164.2 150.0 %all-reduce.9.cloned.1.call-start = ((), (), s32[]{:S(2)}) async-start(), calls=%async_computation.5 | async-start | bytes 8388608 | tf_op jit(solution)/shard_map/psum | solution.py:108
  207.1 213.9 %all-gather.9.cloned.1.call-start = ((), (), s32[]{:S(2)}) async-start(), calls=%async_computation.6 | async-start | bytes 4456448 | tf_op jit(solution)/shard_map/all_gather | solution.py:115
  320.6 106.8 %all-to-all-start = ((bf16[16,256,512]{1,2,0:T(8,128)(2,1)}), bf16[16,256,512]{1,2,0:T(8,128)(2,1)}, u32[]{:S(2)}, u32[]{:S(2)}) async-start(bf16[16,256,512]{1,2,0:T(8,128)(2,1)} %copy.22), calls=%async_computation.1 | async-start | bytes 8388608 | tf_op jit(solution)/shard_map/all_to_all | solution.py:112
  326.2 210.8 %all-reduce.11.cloned.1.call-start = ((), (), s32[]{:S(2)}) async-start(), calls=%async_computation.7 | async-start | bytes 524288 | tf_op jit(solution)/shard_map/psum | solution.py:120
  433.2 222.7 %all-gather.11.cloned.1.call-start = ((), (), s32[]{:S(2)}) async-start(), calls=%async_computation.8 | async-start | bytes 2228224 | tf_op jit(solution)/shard_map/all_gather | solution.py:129
  434.0 193.8 %copy-start.1 = (bf16[192,4096]{1,0:T(8,128)(2,1)S(1)}, bf16[192,4096]{1,0:T(8,128)(2,1)}, u32[]{:S(2)}) copy-start(bf16[192,4096]{1,0:T(8,128)(2,1)} %all-gather.7.cloned.1.call-done) | copy-start | bytes 4718596
  539.9 0.7 copy-start.6
  616.6 15.0 %copy-start.5 = (bf16[256,256]{0,1:T(8,128)(2,1)S(1)}, bf16[256,256]{0,1:T(8,128)(2,1)}, u32[]{:S(2)}) copy-start(bf16[256,256]{0,1:T(8,128)(2,1)} %fusion.19) | copy-start | bytes 393220
Sparse Core Ops, SparseCore 0:
  45.2 44.4 all-gather.4
  93.5 64.4 reduce-scatter.1
  164.4 37.9 all-gather.6
  207.2 106.9 all-reduce.8
  316.4 104.4 all-gather.8
  433.3 103.7 all-reduce.10
  614.1 41.7 all-gather.10
where the time goes:
time: 700 us; the launch traced here: 699 us
  waiting for transfers between devices  466 us (67%)
  other arithmetic  73.8 us (11%)
  blocking collectives  71.5 us (10%)
  matrix products  39.3 us (6%)
  local copies, waits for them, and re-layouts  26.9 us (4%)
  between operations  15.8 us (2%)
    psum x1, waiting for transfers between devices, per_device(): lax.psum(grad_part.astype(jnp.bfloat16), 'dp').astype(jnp.float32)  107 us
    psum x1, waiting for transfers between devices, per_device(): gram_matrix = lax.psum(gram_local, 'fsdp')  103 us
    all_gather x1, waiting for transfers between devices, per_device(): lax.all_gather(right_prev, 'fsdp', axis=0, tiled=True)  94.7 us
    reduce_scatter x1, waiting for transfers between devices, per_device(): lax.psum_scatter(jnp.einsum('cd,ld->cl', weight_rows, cot_cols, preferred...  58.3 us
    all_gather x1, waiting for transfers between devices, per_device(): shard_piece = lax.all_gather(gated_out, 'fsdp', axis=1, tiled=True)  38 us
    another operation x7, other arithmetic, per_device(): lower_factor = jnp.linalg.cholesky(gram_matrix)  36.4 us
    psum x1, blocking collectives, per_device(): square_sums = lax.psum(jnp.sum(x_cols * x_cols, axis=1), 'fsdp')  34.9 us
    all_gather x1, waiting for transfers between devices, per_device(): lax.all_gather(normed_cols, 'fsdp', axis=1, tiled=True)  34.7 us
  transfers between devices with their start and end apart: 8, of which 8 were waited for; matrix products, arithmetic and copies ran while one was open for 6% of the time, Pallas kernels for 0%

commit v1 on v0

v1 whole, which is shorter than its diff:
```python
import functools

import jax
import jax.numpy as jnp
from jax import lax
from jax.experimental import pallas as pl
from jax.experimental.pallas import tpu as pltpu
from jax.sharding import PartitionSpec as P

HIGH = lax.Precision.HIGHEST
F32 = jnp.float32
BF16 = jnp.bfloat16
EXTRA = 16


def exchange(value, axis, size, bits):
    return lax.ppermute(value, axis, [(i, i ^ bits) for i in range(size)])


def plane_gather(piece, size):
    if size != 16:
        whole = lax.all_gather(piece, "fsdp", axis=0)
        quarter = size // 4
        return [whole[i * quarter : (i + 1) * quarter] for i in range(4)]
    send = functools.partial(exchange, axis="fsdp", size=size)
    line = jnp.stack([piece] + [send(piece, bits=4 * step) for step in (1, 2, 3)])
    across = send(line, bits=2)
    return [line, across, send(line, bits=1), send(across, bits=1)]


def plane_order(size):
    if size != 16:
        return jnp.arange(size, dtype=jnp.int32)
    index = lax.axis_index("fsdp").astype(jnp.int32)
    slots = [(bit_x * 2 + bit_core) ^ (4 * step) for bit_core in (0, 1) for bit_x in (0, 1) for step in range(4)]
    return jnp.bitwise_xor(index, jnp.array(slots, jnp.int32))


def plane_sum(value, size):
    if size != 16:
        return lax.psum(value, "fsdp")
    send = functools.partial(exchange, axis="fsdp", size=size)
    value = value + send(value, bits=1)
    value = value + send(value, bits=2)
    return (value + send(value, bits=4)) + (send(value, bits=8) + send(value, bits=12))


def plane_scatter(parts, size):
    index = lax.axis_index("fsdp")
    if size != 16:
        return lax.psum_scatter(parts.astype(F32), "fsdp", scatter_dimension=0, tiled=True)[0]
    rows = parts.shape[1:]
    for bits, lead in ((1, 8), (2, 4), (8, 1), (4, 1)):
        if bits < 4:
            view = parts.reshape((lead, 2) + rows)
            axis, own = 1, (index // bits) % 2
        else:
            count = parts.shape[0]
            view = parts.reshape((2, count // 2) + rows)
            axis, own = 0, (index // bits) % 2
        sent = lax.dynamic_index_in_dim(view, 1 - own, axis, keepdims=False).astype(BF16)
        kept = lax.dynamic_index_in_dim(view, own, axis, keepdims=False).astype(F32)
        parts = kept + exchange(sent, "fsdp", size, bits).astype(F32)
    return parts[0]


def sequences(value, count):
    if count != 2:
        gathered = lax.all_gather(value, "dp", axis=0)
        return [gathered[i] for i in range(count)]
    other = exchange(value, "dp", count, 1)
    first = lax.axis_index("dp") == 0
    return [jnp.where(first, value, other), jnp.where(first, other, value)]


def spread(table, width):
    group = width // table.shape[-2]
    return jnp.repeat(jnp.swapaxes(table, -1, -2), group, axis=-1)


def pad_front(pad, signal):
    length = signal.shape[0]
    pad[pl.ds(0, 8), :] = jnp.zeros((8, signal.shape[1]), F32)
    pad[pl.ds(8, length), :] = signal


def lagged(pad, lag, length):
    return pad[pl.ds(8 - lag, length), :]


def mix_kernel(order, *refs, length, cut, width):
    early, late, weights = refs[0:4], refs[4:8], refs[8:12]
    feat, inner = refs[12:14]
    y_out, qkv_out, saved = refs[14:17]
    acc, factor, pad = refs[17:20]
    step = pl.program_id(0)
    taps = inner.shape[0]

    @pl.when(step == 0)
    def _():
        top = jnp.zeros((cut, 1), F32)
        low = jnp.zeros((length - cut, 1), F32)
        for slot in range(early[0].shape[0]):
            for side in range(4):
                a = early[side][slot].astype(F32)
                b = late[side][slot, : length - cut, :].astype(F32)
                top = top + jnp.sum(a * a, axis=1, keepdims=True)
                low = low + jnp.sum(b * b, axis=1, keepdims=True)
        squares = jnp.concatenate([top, low], axis=0)
        factor[...] = jnp.broadcast_to(lax.rsqrt(squares / width + 1e-05), factor.shape)
        acc[...] = jnp.zeros_like(acc)

    scale = factor[:, 0:1]
    for side in range(4):
        gain = late[side][step, pl.ds(length - cut, EXTRA), :][0:1].astype(F32)
        a = early[side][step].astype(F32)
        b = late[side][step, pl.ds(0, length - cut), :].astype(F32)
        normed = (jnp.concatenate([a, b], axis=0) * scale * gain).astype(BF16)
        for which in range(3):
            acc[which] += lax.dot_general(
                normed, weights[side][which], (((1,), (1,)), ((), ())), preferred_element_type=F32
            )

    @pl.when(step == pl.num_programs(0) - 1)
    def _():
        convs = []
        for which in range(3):
            half = acc[which].astype(BF16)
            qkv_out[which] = half
            pad_front(pad, half.astype(F32))
            total = jnp.zeros((length, acc.shape[2]), F32)
            for lag in range(taps):
                total = total + feat[which, lag : lag + 1, :] * lagged(pad, lag, length)
            convs.append(total)
            saved[which] = total
        gated = convs[1] * convs[2]
        saved[3] = gated
        pad_front(pad, gated)
        window = jnp.zeros(gated.shape, F32)
        for lag in range(taps):
            window = window + inner[lag : lag + 1, :] * lagged(pad, lag, length)
        saved[4] = window
        y_out[...] = (convs[0] * window).astype(BF16)


def mix(order, early, late, w_in, feat, inner):
    slots, cut, width = early[0].shape
    length = cut + late[0].shape[1] - EXTRA
    local = w_in.shape[1]
    taps = inner.shape[0]
    full = lambda shape: pl.BlockSpec(shape, lambda i, o: (0,) * len(shape))
    weight = lambda side: pl.BlockSpec((3, local, width), lambda i, o: (0, 0, o[side * slots + i]))
    return pl.pallas_call(
        functools.partial(mix_kernel, length=length, cut=cut, width=w_in.shape[2]),
        out_shape=(
            jax.ShapeDtypeStruct((length, local), BF16),
            jax.ShapeDtypeStruct((3, length, local), BF16),
            jax.ShapeDtypeStruct((5, length, local), F32),
        ),
        grid_spec=pltpu.PrefetchScalarGridSpec(
            num_scalar_prefetch=1,
            grid=(slots,),
            in_specs=[full(e.shape) for e in early]
            + [full(e.shape) for e in late]
            + [weight(side) for side in range(4)]
            + [full(feat.shape), full(inner.shape)],
            out_specs=(full((length, local)), full((3, length, local)), full((5, length, local))),
            scratch_shapes=[
                pltpu.VMEM((3, length, local), F32),
                pltpu.VMEM((length, 128), F32),
                pltpu.VMEM((length + 16, local), F32),
            ],
        ),
        compiler_params=pltpu.CompilerParams(
            dimension_semantics=("arbitrary",), vmem_limit_bytes=48 * 2**20
        ),
        name="mix",
    )(order, *early, *late, w_in, w_in, w_in, w_in, feat, inner)


def taps_kernel(grad, qkv, saved, inner, pool, out, pad, stack):
    length = grad.shape[0]
    taps = inner.shape[0]
    given = grad[...]
    query_conv, key_conv, value_conv = saved[0], saved[1], saved[2]
    query_grad = given * saved[4]
    window_grad = given * query_conv
    pad[pl.ds(0, length), :] = window_grad
    pad[pl.ds(length, 8), :] = jnp.zeros((8, given.shape[1]), F32)
    gated_grad = jnp.zeros(given.shape, F32)
    for lag in range(taps):
        gated_grad = gated_grad + inner[lag : lag + 1, :] * pad[pl.ds(lag, length), :]
    pairs = (
        (query_grad, qkv[0].astype(F32)),
        (gated_grad * value_conv, qkv[1].astype(F32)),
        (gated_grad * key_conv, qkv[2].astype(F32)),
        (window_grad, saved[3]),
    )
    stack[...] = jnp.zeros_like(stack)
    for row, (gradient, signal) in enumerate(pairs):
        pad_front(pad, signal)
        for lag in range(taps):
            stack[8 * row + lag : 8 * row + lag + 1, :] = jnp.sum(
                gradient * lagged(pad, lag, length), axis=0, keepdims=True
            )
    out[...] = lax.dot_general(
        stack[...], pool[...], (((1,), (0,)), ((), ())), precision=HIGH, preferred_element_type=F32
    )


def filter_taps(grad, qkv, saved, inner, groups):
    length, local = grad.shape
    member = jnp.arange(local)[:, None] // (local // groups) == jnp.arange(groups)[None, :]
    out = pl.pallas_call(
        taps_kernel,
        out_shape=jax.ShapeDtypeStruct((32, groups), F32),
        scratch_shapes=[pltpu.VMEM((length + 16, local), F32), pltpu.VMEM((32, local), F32)],
        name="filter_taps",
    )(grad, qkv, saved, inner, member.astype(F32))
    return jnp.swapaxes(out.reshape(4, 8, groups), 1, 2)[:, :, : inner.shape[0]]


def out_kernel(order, *refs, length):
    sides, weights, x, out, acc = refs[0:4], refs[4:8], refs[8], refs[9], refs[10]
    step = pl.program_id(0)

    @pl.when(step == 0)
    def _():
        acc[...] = jnp.zeros_like(acc)

    total = acc[...]
    for side in range(4):
        total = total + jnp.dot(
            sides[side][0, :length, :], weights[side][...], preferred_element_type=F32
        )
    acc[...] = total

    @pl.when(step == pl.num_programs(0) - 1)
    def _():
        out[...] = (x[...].astype(F32) + total).astype(BF16)


def project(order, sides, w_out, x):
    length, width = x.shape
    slots, rows, local = sides[0].shape
    full = lambda shape: pl.BlockSpec(shape, lambda i, o: (0,) * len(shape))
    weight = lambda side: pl.BlockSpec((local, width), lambda i, o: (o[side * slots + i], 0))
    return pl.pallas_call(
        functools.partial(out_kernel, length=length),
        out_shape=jax.ShapeDtypeStruct((length, width), BF16),
        grid_spec=pltpu.PrefetchScalarGridSpec(
            num_scalar_prefetch=1,
            grid=(slots,),
            in_specs=[pl.BlockSpec((1, rows, local), lambda i, o: (i, 0, 0)) for _ in range(4)]
            + [weight(side) for side in range(4)]
            + [full((length, width))],
            out_specs=full((length, width)),
            scratch_shapes=[pltpu.VMEM((length, width), F32)],
        ),
        compiler_params=pltpu.CompilerParams(dimension_semantics=("arbitrary",)),
        name="project",
    )(order, *sides, w_out, w_out, w_out, w_out, x)


def eliminate(block):
    size = block.shape[0]
    row = lax.broadcasted_iota(jnp.int32, (size, size), 0)
    lane = lax.broadcasted_iota(jnp.int32, (size, size), 1)
    both = jnp.concatenate([block, (row == lane).astype(F32)], axis=1)
    tiles = [both[8 * i : 8 * i + 8, :] for i in range(size // 8)]
    inside = lax.broadcasted_iota(jnp.int32, (8, 1), 0)
    for j in range(size):
        at, off = divmod(j, 8)
        pivot = tiles[at][off : off + 1, :]
        inverse = 1.0 / pivot[:, j : j + 1]
        for i in range(at, size // 8):
            if i == at and off == 7:
                continue
            share = tiles[i][:, j : j + 1] * inverse
            if i == at:
                share = jnp.where(inside > off, share, 0.0)
            tiles[i] = tiles[i] - share * pivot
    both = jnp.concatenate(tiles, axis=0)
    diagonal = jnp.sum(jnp.where(row == lane, both[:, :size], 0.0), axis=1, keepdims=True)
    return both[:, size:] * lax.rsqrt(diagonal)


def dot_high(a, b, contract):
    return lax.dot_general(a, b, (contract, ((), ())), precision=HIGH, preferred_element_type=F32)


def factor_kernel(gram, out):
    half = gram.shape[0] // 2
    first = eliminate(gram[:half, :half])
    below = dot_high(gram[half:, :half], first, ((1,), (1,)))
    rest = gram[half:, half:] - dot_high(below, below, ((1,), (1,)))
    second = eliminate(rest)
    corner = -dot_high(second, dot_high(below, first, ((1,), (0,))), ((1,), (0,)))
    out[:half, :half] = first
    out[:half, half:] = jnp.zeros((half, half), F32)
    out[half:, :half] = corner
    out[half:, half:] = second


def inverse_factor(gram):
    return pl.pallas_call(
        factor_kernel,
        out_shape=jax.ShapeDtypeStruct(gram.shape, F32),
        name="inverse_factor",
    )(gram)


def per_device(ids, embed, gain, w_in, feat_filter, inner_filter, w_out, cotangent, right_prev):
    size = lax.axis_size("fsdp")
    count = lax.axis_size("dp")
    tokens = ids[0]
    length = tokens.shape[0]
    vocab, width = embed.shape
    local = w_in.shape[1]
    rank = right_prev.shape[1]
    cut = length // 2
    order = plane_order(size)

    onehot = (tokens[:, None] == jnp.arange(vocab, dtype=jnp.int32)[None, :]).astype(BF16)
    x_cols = jnp.dot(onehot, embed, preferred_element_type=F32).astype(BF16)
    tail = jnp.broadcast_to(gain[None, :], (EXTRA, width))
    early = plane_gather(x_cols[:cut], size)
    late = plane_gather(jnp.concatenate([x_cols[cut:], tail], axis=0), size)

    cot_cols = cotangent[0]
    parts = jnp.einsum(
        "scd,ld->slc", w_out.reshape(size, local, width), cot_cols, preferred_element_type=F32
    ).astype(BF16)
    side = lax.dot_general(right_prev, cot_cols, (((0,), (1,)), ((), ())), preferred_element_type=F32)
    share = rank // size
    if length <= local:
        packed = jnp.pad(side, ((0, 0), (0, local - length))).reshape(size, share, local)
        summed = plane_scatter(jnp.concatenate([parts, packed.astype(BF16)], axis=1), size)
        y_grad = summed[:length]
        side_own = summed[length:]
        high = side_own.astype(BF16)
        low = (side_own - high.astype(F32)).astype(BF16)
        rider = jnp.concatenate([high, low], axis=0)
    else:
        y_grad = plane_scatter(parts, size)
        rider = jnp.zeros((0, local), BF16)

    feat = spread(feat_filter, local)
    inner = spread(inner_filter, local)
    y, qkv, saved = mix(order, early, late, w_in, feat, inner)

    sent = jnp.concatenate([y, rider], axis=0)
    y_seqs = sequences(sent, count)
    gathered = [plane_gather(piece, size) for piece in y_seqs]
    rows = [jnp.concatenate(sides, axis=0) for sides in gathered]
    mine = lax.axis_index("dp")
    own_sides = [
        lax.dynamic_index_in_dim(jnp.stack([g[i] for g in gathered]), mine, 0, keepdims=False)
        for i in range(4)
    ]
    block_out = project(order, own_sides, w_out, x_cols)[None]

    stacked = jnp.stack([r[:, :length] for r in rows])
    flat = stacked.transpose(0, 2, 1, 3).reshape(count * length, size * local)
    kernel_m = lax.dot_general(flat, flat, (((1,), (1,)), ((), ())), preferred_element_type=F32)
    if length <= local:
        slots = jnp.argsort(order)
        pieces = []
        for r in rows:
            part = r[:, length : length + share].astype(F32) + r[:, length + share :].astype(F32)
            pieces.append(part[slots].reshape(rank, local)[:, :length].T)
        weights = jnp.concatenate(pieces, axis=0)
    else:
        weights = jnp.concatenate(sequences(lax.psum(side, "fsdp").T, count), axis=0)
    product = jnp.dot(kernel_m, weights, precision=HIGH)
    gram = dot_high(weights, product, ((0,), (0,)))
    inverse = inverse_factor(gram) * jnp.sqrt(F32(size * local))
    y_both = jnp.concatenate([p[:length] for p in y_seqs], axis=0).astype(F32)
    panel = dot_high(y_both, weights, ((0,), (0,)))
    basis = dot_high(panel, inverse, ((1,), (1,))).astype(BF16)
    turned = dot_high(product, inverse, ((1,), (1,)))
    cot_both = jnp.concatenate(sequences(cot_cols, count), axis=0).astype(F32)
    right_raw = dot_high(cot_both, turned, ((0,), (0,)))
    column_sums = plane_sum(jnp.sum(right_raw * right_raw, axis=0, keepdims=True), size)
    right_factor = right_raw * lax.rsqrt(column_sums / (size * width) + 1e-06)

    norm_factor = 1.0 / jnp.sqrt(F32(count * length))
    terms = filter_taps(y_grad, qkv, saved, inner, feat_filter.shape[1]) * norm_factor
    halves = sequences(terms.astype(BF16), count)
    filter_grad = sum(h.astype(F32) for h in halves)
    return (block_out, filter_grad, basis, right_factor)


def solution(mesh):
    placed = (
        P("dp", None),
        P(None, "fsdp"),
        P("fsdp"),
        P(None, "fsdp", None),
        P(None, "fsdp", None),
        P("fsdp", None),
        P(None, "fsdp"),
        P("dp", None, "fsdp"),
        P("fsdp", None),
    )
    return jax.shard_map(
        per_device,
        mesh=mesh,
        in_specs=placed,
        out_specs=(P("dp", None, "fsdp"), P(None, "fsdp", None), P("fsdp", None), P("fsdp", None)),
        check_vma=False,
    )
```

time: 700 us -> 174 us (0.25)
  waiting for transfers between devices: 466 us -> 42 us
  blocking collectives: 71.5 us -> 0 us
  other arithmetic: 73.8 us -> 13.2 us
  Pallas kernels: 0 us -> 43.2 us
  starting transfers between devices: 6.13 us -> 46.6 us
  matrix products: 39.3 us -> 14.4 us
  between operations: 15.8 us -> 1.31 us
  local copies, waits for them, and re-layouts: 26.9 us -> 12.8 us
    psum x2 -> x0, waiting for transfers between devices: 210 us -> none  [the longest x1 107 us: per_device(): lax.psum(grad_part.astype(jnp.bfloat16), 'dp').astype(jnp.float32)]
    all_gather x4 -> x0, waiting for transfers between devices: 191 us -> none  [the longest x1 94.7 us: per_device(): lax.all_gather(right_prev, 'fsdp', axis=0, tiled=True)]
    psum x3 -> x0, blocking collectives: 71.5 us -> none  [the longest x1 34.9 us: per_device(): square_sums = lax.psum(jnp.sum(x_cols * x_cols, axis=1), 'fsdp')]
    another operation x10 -> x5, other arithmetic: 59.2 us -> 0.28 us  [plane_gather(): jnp.stack([piece] + [send(piece, bits=4 * step) for step in (1, 2, 3)])]
    reduce_scatter x1 -> x0, waiting for transfers between devices: 58.3 us -> none  [per_device(): lax.psum_scatter(jnp.einsum('cd,ld->cl', weight_rows, cot_cols, preferred...]
    ppermute x0 -> x36, starting transfers between devices: none -> 46.6 us  [exchange(): return lax.ppermute(value, axis, [(i, i ^ bits) for i in range(size)])]
    pallas_call x0 -> x4, Pallas kernels: none -> 43.2 us  [the longest x1 24 us: inverse_factor(): pl.pallas_call(factor_kernel, out_shape=jax.ShapeDtypeStruct(gram.shape,...]
    ppermute x0 -> x36, waiting for transfers between devices: none -> 42 us  [exchange(): return lax.ppermute(value, axis, [(i, i ^ bits) for i in range(size)])]
  transfers between devices with their start and end apart: 8 -> 36, of which waited for: 8 -> 12; matrix products, arithmetic and copies ran while one was open for 6% -> 7% of each run, Pallas kernels for 0% -> 9%
where the time goes in v1:
time: 174 us
  starting transfers between devices  46.6 us (27%)
  Pallas kernels  43.2 us (25%)
  waiting for transfers between devices  42 us (24%)
  matrix products  14.4 us (8%)
  other arithmetic  13.2 us (8%)
  local copies, waits for them, and re-layouts  12.8 us (7%)
    ppermute x36, starting transfers between devices, exchange(): return lax.ppermute(value, axis, [(i, i ^ bits) for i in range(size)])  46.6 us
    ppermute x36, waiting for transfers between devices, exchange(): return lax.ppermute(value, axis, [(i, i ^ bits) for i in range(size)])  42 us
    pallas_call x1, Pallas kernels, inverse_factor(): pl.pallas_call(factor_kernel, out_shape=jax.ShapeDtypeStruct(gram.shape,...  24 us
    pallas_call x1, Pallas kernels, mix(): pl.pallas_call(functools.partial(mix_kernel, length=length, cut=cut, widt...  10.1 us
    pallas_call x1, Pallas kernels, project(): pl.pallas_call(functools.partial(out_kernel, length=length), out_shape=ja...  5.75 us
    dot_general x5, matrix products, dot_high(): lax.dot_general(a, b, (contract, ((), ())), precision=HIGH, preferred_ele...  5.09 us
    dot_general x1, matrix products, per_device(): jnp.einsum('scd,ld->slc', w_out.reshape(size, local, width), cot_cols, pr...  4.99 us
    squeeze x4, other arithmetic, per_device(): lax.dynamic_index_in_dim(jnp.stack([g[i] for g in gathered]), mine, 0, ke...  3.81 us
  transfers between devices with their start and end apart: 36, of which 12 were waited for; matrix products, arithmetic and copies ran while one was open for 7% of the time, Pallas kernels for 9%

profile of v1, /device:TPU:0, one launch (start us, length us, event | category | flops | bytes accessed | tf_op | source)
XLA Modules:
  0.0 173.5 jit_solution(9417417662655589385)
XLA Ops:
  2.1 5.0 %fusion = bf16[16,192,256]{2,1,0:T(8,128)(2,1)} fusion(bf16[16,256,512]{2,1,0:T(8,128)(2,1)} %bitcast.120, bf16[1,192,512]{2,1,0:T(8,128)(2,1)} %param.17), kind=kOutput, calls=%fused_computation.8 | convolution fusion | flops 806092800 | bytes 5963776 | tf_op jit(solution)/shard_map/scd,ld->slc/dot_general | solution.py:331
  10.5 3.7 %collective-permute-start.1 = (bf16[96,512]{1,0:T(8,128)(2,1)S(1)}, bf16[96,512]{1,0:T(8,128)(2,1)S(1)}, u32[]{:S(2)}, u32[]{:S(2)}) collective-permute-start(bf16[96,512]{1,0:T(8,128)(2,1)S(1)} %get-tuple-element.28), channel_id=1, source_target_pairs={{0,8},{1,9},{2,10},{3,11},{4,12},{5,13},{6,14},{7,15},{8,0},{9,1},... | collective-permute-start | bytes 294920 | tf_op jit(solution)/shard_map/ppermute | solution.py:17
  15.8 2.0 %collective-permute-start.7 = (bf16[112,512]{1,0:T(8,128)(2,1)S(1)}, bf16[112,512]{1,0:T(8,128)(2,1)S(1)}, u32[]{:S(2)}, u32[]{:S(2)}) collective-permute-start(bf16[112,512]{1,0:T(8,128)(2,1)S(1)} %get-tuple-element.30), channel_id=1, source_target_pairs={{0,8},{1,9},{2,10},{3,11},{4,12},{5,13},{6,14},{7,15},{8,0},{9,1},... | collective-permute-start | bytes 344072 | tf_op jit(solution)/shard_map/ppermute | solution.py:17
  22.5 2.5 %collective-permute-start.6 = (bf16[112,512]{1,0:T(8,128)(2,1)S(1)}, bf16[112,512]{1,0:T(8,128)(2,1)S(1)}, u32[]{:S(2)}, u32[]{:S(2)}) collective-permute-start(bf16[112,512]{1,0:T(8,128)(2,1)S(1)} %get-tuple-element.30), channel_id=1, source_target_pairs={{0,4},{1,5},{2,6},{3,7},{4,0},{5,1},{6,2},{7,3},{8,12},{9,13},{10,... | collective-permute-start | bytes 344072 | tf_op jit(solution)/shard_map/ppermute | solution.py:17
  26.9 3.4 %collective-permute-done.7 = bf16[112,512]{1,0:T(8,128)(2,1)S(1)} collective-permute-done((bf16[112,512]{1,0:T(8,128)(2,1)S(1)}, bf16[112,512]{1,0:T(8,128)(2,1)S(1)}, u32[]{:S(2)}, u32[]{:S(2)}) %collective-permute-start.7) | collective-permute-done | bytes 114720 | tf_op jit(solution)/shard_map/ppermute | solution.py:17
  30.3 3.0 %collective-permute-start.3 = (bf16[4,96,512]{2,1,0:T(8,128)(2,1)S(1)}, bf16[4,96,512]{2,1,0:T(8,128)(2,1)S(1)}, u32[]{:S(2)}, u32[]{:S(2)}) collective-permute-start(bf16[4,96,512]{2,1,0:T(8,128)(2,1)S(1)} %pad_maximum_fusion.4.refs_0_), channel_id=1, source_target_pairs={{0,2},{1,3},{2,0},{3,1},{4,6},{5,7},{6,4},{7,5},{8,10},{9,11},{10,... | collective-permute-start | bytes 1179656 | tf_op jit(solution)/shard_map/ppermute | solution.py:17
  33.6 4.7 %collective-permute-start.14 = (bf16[2,208,256]{2,1,0:T(8,128)(2,1)S(1)}, bf16[2,208,256]{2,1,0:T(8,128)(2,1)S(1)}, u32[]{:S(2)}, u32[]{:S(2)}) collective-permute-start(bf16[2,208,256]{2,1,0:T(8,128)(2,1)S(1)} %fusion.17), channel_id=1, source_target_pairs={{0,8},{1,9},{2,10},{3,11},{4,12},{5,13},{6,14},{7,15},{8,0},{9,1},... | collective-permute-start | bytes 638984 | tf_op jit(solution)/shard_map/ppermute | solution.py:17
  39.0 4.3 %collective-permute-done.3.refs_1_ = bf16[4,96,512]{2,1,0:T(8,128)(2,1)S(1)} collective-permute-done((bf16[4,96,512]{2,1,0:T(8,128)(2,1)S(1)}, bf16[4,96,512]{2,1,0:T(8,128)(2,1)S(1)}, u32[]{:S(2)}, u32[]{:S(2)}) %collective-permute-start.3) | collective-permute-done | bytes 393248 | tf_op jit(solution)/shard_map/ppermute | solution.py:17
  43.3 8.4 %collective-permute-done.9.refs_5_ = bf16[4,112,512]{2,1,0:T(8,128)(2,1)S(1)} collective-permute-done((bf16[4,112,512]{2,1,0:T(8,128)(2,1)S(1)}, bf16[4,112,512]{2,1,0:T(8,128)(2,1)S(1)}, u32[]{:S(2)}, u32[]{:S(2)}) %collective-permute-start.9) | collective-permute-done | bytes 458784 | tf_op jit(solution)/shard_map/ppermute | solution.py:17
  54.5 10.1 %mix.1 = (bf16[192,256]{1,0:T(8,128)(2,1)S(1)}, bf16[3,192,256]{2,1,0:T(8,128)(2,1)S(1)}, f32[5,192,256]{2,1,0:T(8,128)S(1)}) custom-call(s32[16]{0:T(128)S(1)} %broadcast_xor_fusion.order, bf16[4,96,512]{2,1,0:T(8,128)(2,1)S(1)} %pad_maximum_fusion.4.refs_0_, bf16[4,96,512]{2,1,0:T(8,128)(2,1)S(1)} %collective-permute-done.3.refs_1_, ...), custom_call_target="tpu_custom_call" | custom-call | tf_op jit(solution)/shard_map/mix/pallas_call | solution.py:153
  67.0 3.3 %filter_taps.1 = f32[32,16]{1,0:T(8,128)} custom-call(f32[192,256]{1,0:T(8,128)} %slice_bitcast_fusion.4.grad, bf16[3,192,256]{2,1,0:T(8,128)(2,1)} %copy-done.2, f32[5,192,256]{2,1,0:T(8,128)} %copy-done.1, f32[7,256]{1,0:T(8,128)} %copy-done.3, f32[256,16]{1,0:T(8,128)} %fusion.26.pool), custom_call_target="tpu_custom_call" | custom-call | tf_op jit(solution)/shard_map/filter_taps/pallas_call | solution.py:214
  73.1 2.9 %collective-permute-done.16 = bf16[224,256]{1,0:T(8,128)(2,1)S(1)} collective-permute-done((bf16[224,256]{1,0:T(8,128)(2,1)S(1)}, bf16[224,256]{1,0:T(8,128)(2,1)S(1)}, u32[]{:S(2)}, u32[]{:S(2)}) %collective-permute-start.16) | collective-permute-done | bytes 114720 | tf_op jit(solution)/shard_map/ppermute | solution.py:17
  76.1 4.1 %collective-permute-start.22 = (bf16[224,256]{1,0:T(8,128)(2,1)S(1)}, bf16[224,256]{1,0:T(8,128)(2,1)S(1)}, u32[]{:S(2)}, u32[]{:S(2)}) collective-permute-start(bf16[224,256]{1,0:T(8,128)(2,1)S(1)} %get-tuple-element.15), channel_id=1, source_target_pairs={{0,12},{1,13},{2,14},{3,15},{4,8},{5,9},{6,10},{7,11},{8,4},{9,5},... | collective-permute-start | bytes 344072 | tf_op jit(solution)/shard_map/ppermute | solution.py:17
  82.7 3.7 %collective-permute-start.19 = (bf16[224,256]{1,0:T(8,128)(2,1)S(1)}, bf16[224,256]{1,0:T(8,128)(2,1)S(1)}, u32[]{:S(2)}, u32[]{:S(2)}) collective-permute-start(bf16[224,256]{1,0:T(8,128)(2,1)S(1)} %get-tuple-element.25), channel_id=1, source_target_pairs={{0,12},{1,13},{2,14},{3,15},{4,8},{5,9},{6,10},{7,11},{8,4},{9,5},... | collective-permute-start | bytes 344072 | tf_op jit(solution)/shard_map/ppermute | solution.py:17
  86.5 3.3 %collective-permute-start.17 = (bf16[224,256]{1,0:T(8,128)(2,1)S(1)}, bf16[224,256]{1,0:T(8,128)(2,1)S(1)}, u32[]{:S(2)}, u32[]{:S(2)}) collective-permute-start(bf16[224,256]{1,0:T(8,128)(2,1)S(1)} %get-tuple-element.25), channel_id=1, source_target_pairs={{0,4},{1,5},{2,6},{3,7},{4,0},{5,1},{6,2},{7,3},{8,12},{9,13},{10,... | collective-permute-start | bytes 344072 | tf_op jit(solution)/shard_map/ppermute | solution.py:17
  89.7 5.2 %collective-permute-done.21 = bf16[224,256]{1,0:T(8,128)(2,1)S(1)} collective-permute-done((bf16[224,256]{1,0:T(8,128)(2,1)S(1)}, bf16[224,256]{1,0:T(8,128)(2,1)S(1)}, u32[]{:S(2)}, u32[]{:S(2)}) %collective-permute-start.21) | collective-permute-done | bytes 114720 | tf_op jit(solution)/shard_map/ppermute | solution.py:17
  96.6 2.1 %collective-permute-done.18 = bf16[224,256]{1,0:T(8,128)(2,1)S(1)} collective-permute-done((bf16[224,256]{1,0:T(8,128)(2,1)S(1)}, bf16[224,256]{1,0:T(8,128)(2,1)S(1)}, u32[]{:S(2)}, u32[]{:S(2)}) %collective-permute-start.18) | collective-permute-done | bytes 114720 | tf_op jit(solution)/shard_map/ppermute | solution.py:17
  101.4 6.2 %collective-permute-done.24 = bf16[4,224,256]{2,1,0:T(8,128)(2,1)S(1)} collective-permute-done((bf16[4,224,256]{2,1,0:T(8,128)(2,1)S(1)}, bf16[4,224,256]{2,1,0:T(8,128)(2,1)S(1)}, u32[]{:S(2)}, u32[]{:S(2)}) %collective-permute-start.24) | collective-permute-done | bytes 458784 | tf_op jit(solution)/shard_map/ppermute | solution.py:17
  107.6 6.3 %collective-permute-done.23 = bf16[4,224,256]{2,1,0:T(8,128)(2,1)S(1)} collective-permute-done((bf16[4,224,256]{2,1,0:T(8,128)(2,1)S(1)}, bf16[4,224,256]{2,1,0:T(8,128)(2,1)S(1)}, u32[]{:S(2)}, u32[]{:S(2)}) %collective-permute-start.23) | collective-permute-done | bytes 458784 | tf_op jit(solution)/shard_map/ppermute | solution.py:17
  123.1 1.8 %copy.19 = bf16[2,192,16,256]{3,2,1,0:T(8,128)(2,1)S(1)} copy(bf16[2,192,16,256]{3,1,2,0:T(8,128)(2,1)S(1)} %maximum_bitcast_fusion) | data formatting | bytes 6291456 | tf_op jit(solution)/shard_map/transpose | solution.py:364
  126.4 1.8 %fusion.44 = f32[384,384]{1,0:T(8,128)S(1)} fusion(bf16[384,4096]{1,0:T(8,128)(2,1)S(1)} %bitcast.126), kind=kOutput, calls=%fused_computation.117 | convolution fusion | flops 1207959552 | bytes 3735552 | tf_op jit(solution)/shard_map/dot_general | solution.py:365
  130.5 24.0 %inverse_factor.1 = f32[256,256]{1,0:T(8,128)} custom-call(f32[256,256]{1,0:T(8,128)} %fusion.27.gram), custom_call_target="tpu_custom_call" | custom-call | tf_op jit(solution)/shard_map/inverse_factor/pallas_call | solution.py:306
  161.6 3.2 %collective-permute-start.35 = (f32[1,256]{1,0:T(1,128)S(1)}, f32[1,256]{1,0:T(1,128)S(1)}, u32[]{:S(2)}, u32[]{:S(2)}) collective-permute-start(f32[1,256]{1,0:T(1,128)S(1)} %add.132), channel_id=1, source_target_pairs={{0,12},{1,13},{2,14},{3,15},{4,8},{5,9},{6,10},{7,11},{8,4},{9,5},... | collective-permute-start | bytes 3080 | tf_op jit(solution)/shard_map/ppermute | solution.py:17
  166.9 5.8 %project.1 = bf16[192,512]{1,0:T(8,128)(2,1)} custom-call(s32[16]{0:T(128)} %copy-done.4, bf16[4,224,256]{2,1,0:T(8,128)(2,1)} %fusion.8.refs_0_, bf16[4,224,256]{2,1,0:T(8,128)(2,1)} %fusion.6.refs_1_, bf16[4,224,256]{2,1,0:T(8,128)(2,1)} %fusion.4.refs_2_, bf16[4,224,256]{2,1,0:T(8,128)(2,1)} %fusion.2.refs_3_, bf16[4096,512]{1,0:T(8,128)(2,1)} %refs_7_.1, ...), custom_call_target="tpu_custom_call" | custom-call | tf_op jit(solution)/shard_map/project/pallas_call | solution.py:248
  (167 shorter events, 51.5 us)
Async XLA Ops:
  9.7 9.8 %collective-permute-start.12 = (bf16[8,208,256]{2,1,0:T(8,128)(2,1)}, bf16[8,208,256]{2,1,0:T(8,128)(2,1)}, u32[]{:S(2)}, u32[]{:S(2)}) collective-permute-start(bf16[8,208,256]{2,1,0:T(8,128)(2,1)} %dynamic-slice_bitcast_fusion), channel_id=1, source_target_pairs={{0,1},{1,0},{2,3},{3,2},{4,5},{5,4},{6,7},{7,6},{8,9},{9,8},{10,11... | collective-permute-start | bytes 2555912 | tf_op jit(solution)/shard_map/ppermute | solution.py:17
  10.5 12.0 %collective-permute-start.1 = (bf16[96,512]{1,0:T(8,128)(2,1)S(1)}, bf16[96,512]{1,0:T(8,128)(2,1)S(1)}, u32[]{:S(2)}, u32[]{:S(2)}) collective-permute-start(bf16[96,512]{1,0:T(8,128)(2,1)S(1)} %get-tuple-element.28), channel_id=1, source_target_pairs={{0,8},{1,9},{2,10},{3,11},{4,12},{5,13},{6,14},{7,15},{8,0},{9,1},... | collective-permute-start | bytes 294920 | tf_op jit(solution)/shard_map/ppermute | solution.py:17
  14.2 10.9 %collective-permute-start = (bf16[96,512]{1,0:T(8,128)(2,1)S(1)}, bf16[96,512]{1,0:T(8,128)(2,1)S(1)}, u32[]{:S(2)}, u32[]{:S(2)}) collective-permute-start(bf16[96,512]{1,0:T(8,128)(2,1)S(1)} %get-tuple-element.28), channel_id=1, source_target_pairs={{0,4},{1,5},{2,6},{3,7},{4,0},{5,1},{6,2},{7,3},{8,12},{9,13},{10,... | collective-permute-start | bytes 294920 | tf_op jit(solution)/shard_map/ppermute | solution.py:17
  15.8 14.5 %collective-permute-start.7 = (bf16[112,512]{1,0:T(8,128)(2,1)S(1)}, bf16[112,512]{1,0:T(8,128)(2,1)S(1)}, u32[]{:S(2)}, u32[]{:S(2)}) collective-permute-start(bf16[112,512]{1,0:T(8,128)(2,1)S(1)} %get-tuple-element.30), channel_id=1, source_target_pairs={{0,8},{1,9},{2,10},{3,11},{4,12},{5,13},{6,14},{7,15},{8,0},{9,1},... | collective-permute-start | bytes 344072 | tf_op jit(solution)/shard_map/ppermute | solution.py:17
  21.0 12.5 %collective-permute-start.13 = (bf16[4,208,256]{2,1,0:T(8,128)(2,1)S(1)}, bf16[4,208,256]{2,1,0:T(8,128)(2,1)S(1)}, u32[]{:S(2)}, u32[]{:S(2)}) collective-permute-start(bf16[4,208,256]{2,1,0:T(8,128)(2,1)S(1)} %fusion.9), channel_id=1, source_target_pairs={{0,2},{1,3},{2,0},{3,1},{4,6},{5,7},{6,4},{7,5},{8,10},{9,11},{10,... | collective-permute-start | bytes 1277960 | tf_op jit(solution)/shard_map/ppermute | solution.py:17
  22.5 10.7 %collective-permute-start.6 = (bf16[112,512]{1,0:T(8,128)(2,1)S(1)}, bf16[112,512]{1,0:T(8,128)(2,1)S(1)}, u32[]{:S(2)}, u32[]{:S(2)}) collective-permute-start(bf16[112,512]{1,0:T(8,128)(2,1)S(1)} %get-tuple-element.30), channel_id=1, source_target_pairs={{0,4},{1,5},{2,6},{3,7},{4,0},{5,1},{6,2},{7,3},{8,12},{9,13},{10,... | collective-permute-start | bytes 344072 | tf_op jit(solution)/shard_map/ppermute | solution.py:17
  25.3 27.0 %collective-permute-start.30 = (bf16[192,512]{1,0:T(8,128)(2,1)S(1)}, bf16[192,512]{1,0:T(8,128)(2,1)S(1)}, u32[]{:S(2)}, u32[]{:S(2)}) collective-permute-start(bf16[192,512]{1,0:T(8,128)(2,1)S(1)} %bitcast.135), channel_id=1, source_target_pairs={{0,16},{16,0},{1,17},{17,1},{2,18},{18,2},{3,19},{19,3},{4,20},{20... | collective-permute-start | bytes 589832 | tf_op jit(solution)/shard_map/ppermute | solution.py:17
  30.3 13.0 %collective-permute-start.3 = (bf16[4,96,512]{2,1,0:T(8,128)(2,1)S(1)}, bf16[4,96,512]{2,1,0:T(8,128)(2,1)S(1)}, u32[]{:S(2)}, u32[]{:S(2)}) collective-permute-start(bf16[4,96,512]{2,1,0:T(8,128)(2,1)S(1)} %pad_maximum_fusion.4.refs_0_), channel_id=1, source_target_pairs={{0,2},{1,3},{2,0},{3,1},{4,6},{5,7},{6,4},{7,5},{8,10},{9,11},{10,... | collective-permute-start | bytes 1179656 | tf_op jit(solution)/shard_map/ppermute | solution.py:17
  33.3 18.4 %collective-permute-start.9 = (bf16[4,112,512]{2,1,0:T(8,128)(2,1)S(1)}, bf16[4,112,512]{2,1,0:T(8,128)(2,1)S(1)}, u32[]{:S(2)}, u32[]{:S(2)}) collective-permute-start(bf16[4,112,512]{2,1,0:T(8,128)(2,1)S(1)} %pad_maximum_fusion.1.refs_4_), channel_id=1, source_target_pairs={{0,2},{1,3},{2,0},{3,1},{4,6},{5,7},{6,4},{7,5},{8,10},{9,11},{10,... | collective-permute-start | bytes 1376264 | tf_op jit(solution)/shard_map/ppermute | solution.py:17
  33.6 18.1 %collective-permute-start.14 = (bf16[2,208,256]{2,1,0:T(8,128)(2,1)S(1)}, bf16[2,208,256]{2,1,0:T(8,128)(2,1)S(1)}, u32[]{:S(2)}, u32[]{:S(2)}) collective-permute-start(bf16[2,208,256]{2,1,0:T(8,128)(2,1)S(1)} %fusion.17), channel_id=1, source_target_pairs={{0,8},{1,9},{2,10},{3,11},{4,12},{5,13},{6,14},{7,15},{8,0},{9,1},... | collective-permute-start | bytes 638984 | tf_op jit(solution)/shard_map/ppermute | solution.py:17
  39.0 15.4 %collective-permute-start.4 = (bf16[4,96,512]{2,1,0:T(8,128)(2,1)S(1)}, bf16[4,96,512]{2,1,0:T(8,128)(2,1)S(1)}, u32[]{:S(2)}, u32[]{:S(2)}) collective-permute-start(bf16[4,96,512]{2,1,0:T(8,128)(2,1)S(1)} %pad_maximum_fusion.4.refs_0_), channel_id=1, source_target_pairs={{0,1},{1,0},{2,3},{3,2},{4,5},{5,4},{6,7},{7,6},{8,9},{9,8},{10,11... | collective-permute-start | bytes 1179656 | tf_op jit(solution)/shard_map/ppermute | solution.py:17
  43.3 11.1 %collective-permute-start.10 = (bf16[4,112,512]{2,1,0:T(8,128)(2,1)S(1)}, bf16[4,112,512]{2,1,0:T(8,128)(2,1)S(1)}, u32[]{:S(2)}, u32[]{:S(2)}) collective-permute-start(bf16[4,112,512]{2,1,0:T(8,128)(2,1)S(1)} %pad_maximum_fusion.1.refs_4_), channel_id=1, source_target_pairs={{0,1},{1,0},{2,3},{3,2},{4,5},{5,4},{6,7},{7,6},{8,9},{9,8},{10,11... | collective-permute-start | bytes 1376264 | tf_op jit(solution)/shard_map/ppermute | solution.py:17
  52.3 13.9 %collective-permute-start.15 = (bf16[1,208,256]{2,1,0:T(8,128)(2,1)S(1)}, bf16[1,208,256]{2,1,0:T(8,128)(2,1)S(1)}, u32[]{:S(2)}, u32[]{:S(2)}) collective-permute-start(bf16[1,208,256]{2,1,0:T(8,128)(2,1)S(1)} %dynamic-slice_convert_fusion.2), channel_id=1, source_target_pairs={{0,4},{1,5},{2,6},{3,7},{4,0},{5,1},{6,2},{7,3},{8,12},{9,13},{10,... | collective-permute-start | bytes 319496 | tf_op jit(solution)/shard_map/ppermute | solution.py:17
  76.1 10.4 %collective-permute-start.22 = (bf16[224,256]{1,0:T(8,128)(2,1)S(1)}, bf16[224,256]{1,0:T(8,128)(2,1)S(1)}, u32[]{:S(2)}, u32[]{:S(2)}) collective-permute-start(bf16[224,256]{1,0:T(8,128)(2,1)S(1)} %get-tuple-element.15), channel_id=1, source_target_pairs={{0,12},{1,13},{2,14},{3,15},{4,8},{5,9},{6,10},{7,11},{8,4},{9,5},... | collective-permute-start | bytes 344072 | tf_op jit(solution)/shard_map/ppermute | solution.py:17
  80.2 14.7 %collective-permute-start.21 = (bf16[224,256]{1,0:T(8,128)(2,1)S(1)}, bf16[224,256]{1,0:T(8,128)(2,1)S(1)}, u32[]{:S(2)}, u32[]{:S(2)}) collective-permute-start(bf16[224,256]{1,0:T(8,128)(2,1)S(1)} %get-tuple-element.15), channel_id=1, source_target_pairs={{0,8},{1,9},{2,10},{3,11},{4,12},{5,13},{6,14},{7,15},{8,0},{9,1},... | collective-permute-start | bytes 344072 | tf_op jit(solution)/shard_map/ppermute | solution.py:17
  80.2 14.7 %collective-permute-start.20 = (bf16[224,256]{1,0:T(8,128)(2,1)S(1)}, bf16[224,256]{1,0:T(8,128)(2,1)S(1)}, u32[]{:S(2)}, u32[]{:S(2)}) collective-permute-start(bf16[224,256]{1,0:T(8,128)(2,1)S(1)} %get-tuple-element.15), channel_id=1, source_target_pairs={{0,4},{1,5},{2,6},{3,7},{4,0},{5,1},{6,2},{7,3},{8,12},{9,13},{10,... | collective-permute-start | bytes 344072 | tf_op jit(solution)/shard_map/ppermute | solution.py:17
  82.7 13.8 %collective-permute-start.19 = (bf16[224,256]{1,0:T(8,128)(2,1)S(1)}, bf16[224,256]{1,0:T(8,128)(2,1)S(1)}, u32[]{:S(2)}, u32[]{:S(2)}) collective-permute-start(bf16[224,256]{1,0:T(8,128)(2,1)S(1)} %get-tuple-element.25), channel_id=1, source_target_pairs={{0,12},{1,13},{2,14},{3,15},{4,8},{5,9},{6,10},{7,11},{8,4},{9,5},... | collective-permute-start | bytes 344072 | tf_op jit(solution)/shard_map/ppermute | solution.py:17
  86.5 12.2 %collective-permute-start.18 = (bf16[224,256]{1,0:T(8,128)(2,1)S(1)}, bf16[224,256]{1,0:T(8,128)(2,1)S(1)}, u32[]{:S(2)}, u32[]{:S(2)}) collective-permute-start(bf16[224,256]{1,0:T(8,128)(2,1)S(1)} %get-tuple-element.25), channel_id=1, source_target_pairs={{0,8},{1,9},{2,10},{3,11},{4,12},{5,13},{6,14},{7,15},{8,0},{9,1},... | collective-permute-start | bytes 344072 | tf_op jit(solution)/shard_map/ppermute | solution.py:17
  86.5 12.2 %collective-permute-start.17 = (bf16[224,256]{1,0:T(8,128)(2,1)S(1)}, bf16[224,256]{1,0:T(8,128)(2,1)S(1)}, u32[]{:S(2)}, u32[]{:S(2)}) collective-permute-start(bf16[224,256]{1,0:T(8,128)(2,1)S(1)} %get-tuple-element.25), channel_id=1, source_target_pairs={{0,4},{1,5},{2,6},{3,7},{4,0},{5,1},{6,2},{7,3},{8,12},{9,13},{10,... | collective-permute-start | bytes 344072 | tf_op jit(solution)/shard_map/ppermute | solution.py:17
  95.0 12.6 %collective-permute-start.24 = (bf16[4,224,256]{2,1,0:T(8,128)(2,1)S(1)}, bf16[4,224,256]{2,1,0:T(8,128)(2,1)S(1)}, u32[]{:S(2)}, u32[]{:S(2)}) collective-permute-start(bf16[4,224,256]{2,1,0:T(8,128)(2,1)S(1)} %get-tuple-element.18), channel_id=1, source_target_pairs={{0,2},{1,3},{2,0},{3,1},{4,6},{5,7},{6,4},{7,5},{8,10},{9,11},{10,... | collective-permute-start | bytes 1376264 | tf_op jit(solution)/shard_map/ppermute | solution.py:17
  96.6 18.3 %collective-permute-start.26 = (bf16[4,224,256]{2,1,0:T(8,128)(2,1)S(1)}, bf16[4,224,256]{2,1,0:T(8,128)(2,1)S(1)}, u32[]{:S(2)}, u32[]{:S(2)}) collective-permute-start(bf16[4,224,256]{2,1,0:T(8,128)(2,1)S(1)} %get-tuple-element.18), channel_id=1, source_target_pairs={{0,1},{1,0},{2,3},{3,2},{4,5},{5,4},{6,7},{7,6},{8,9},{9,8},{10,11... | collective-permute-start | bytes 1376264 | tf_op jit(solution)/shard_map/ppermute | solution.py:17
  98.8 15.1 %collective-permute-start.23 = (bf16[4,224,256]{2,1,0:T(8,128)(2,1)S(1)}, bf16[4,224,256]{2,1,0:T(8,128)(2,1)S(1)}, u32[]{:S(2)}, u32[]{:S(2)}) collective-permute-start(bf16[4,224,256]{2,1,0:T(8,128)(2,1)S(1)} %get-tuple-element.20), channel_id=1, source_target_pairs={{0,2},{1,3},{2,0},{3,1},{4,6},{5,7},{6,4},{7,5},{8,10},{9,11},{10,... | collective-permute-start | bytes 1376264 | tf_op jit(solution)/shard_map/ppermute | solution.py:17
  100.3 14.5 %collective-permute-start.25 = (bf16[4,224,256]{2,1,0:T(8,128)(2,1)S(1)}, bf16[4,224,256]{2,1,0:T(8,128)(2,1)S(1)}, u32[]{:S(2)}, u32[]{:S(2)}) collective-permute-start(bf16[4,224,256]{2,1,0:T(8,128)(2,1)S(1)} %get-tuple-element.20), channel_id=1, source_target_pairs={{0,1},{1,0},{2,3},{3,2},{4,5},{5,4},{6,7},{7,6},{8,9},{9,8},{10,11... | collective-permute-start | bytes 1376264 | tf_op jit(solution)/shard_map/ppermute | solution.py:17
  161.6 11.1 %collective-permute-start.35 = (f32[1,256]{1,0:T(1,128)S(1)}, f32[1,256]{1,0:T(1,128)S(1)}, u32[]{:S(2)}, u32[]{:S(2)}) collective-permute-start(f32[1,256]{1,0:T(1,128)S(1)} %add.132), channel_id=1, source_target_pairs={{0,12},{1,13},{2,14},{3,15},{4,8},{5,9},{6,10},{7,11},{8,4},{9,5},... | collective-permute-start | bytes 3080 | tf_op jit(solution)/shard_map/ppermute | solution.py:17
  (30 other events, 317.4 us)

commit v2 on v1

--- a/solution.py
+++ b/solution.py
@@ -1,4 +1,5 @@
 import functools
+import math
 
 import jax
 import jax.numpy as jnp
@@ -42,7 +43,8 @@
     send = functools.partial(exchange, axis="fsdp", size=size)
     value = value + send(value, bits=1)
     value = value + send(value, bits=2)
-    return (value + send(value, bits=4)) + (send(value, bits=8) + send(value, bits=12))
+    value = value + send(value, bits=4)
+    return value + send(value, bits=8)
 
 
 def plane_scatter(parts, size):
@@ -262,27 +264,73 @@
     )(order, *sides, w_out, w_out, w_out, w_out, x)
 
 
+def out_whole_kernel(order, *refs, length, local):
+    count = len(RELATIVE)
+    pieces, weights, x, out = refs[:count], refs[count], refs[count + 1], refs[count + 2]
+    here, sems = refs[count + 3 :]
+    for copy in copies_in(weights, here, sems):
+        copy.wait()
+    total = x[:length, :].astype(F32)
+    for slot, piece in enumerate(pieces):
+        place = pl.ds(pl.multiple_of(order[slot] * local, local), local)
+        total = total + jnp.dot(piece[:length, :], here[place, :], preferred_element_type=F32)
+    out[...] = total.astype(BF16)
+
+
+def project_whole(order, pieces, w_out, x):
+    width = x.shape[1]
+    length = x.shape[0] - EXTRA
+    local = pieces[0].shape[1]
+    whole = pl.BlockSpec(memory_space=pltpu.VMEM)
+    return pl.pallas_call(
+        functools.partial(out_whole_kernel, length=length, local=local),
+        out_shape=jax.ShapeDtypeStruct((length, width), BF16),
+        in_specs=[pl.BlockSpec(memory_space=pltpu.SMEM)]
+        + [whole] * len(pieces)
+        + [pl.BlockSpec(memory_space=pltpu.HBM), whole],
+        out_specs=whole,
+        scratch_shapes=[pltpu.VMEM(w_out.shape, w_out.dtype), pltpu.SemaphoreType.DMA((8,))],
+        compiler_params=pltpu.CompilerParams(vmem_limit_bytes=16 * 2**20),
+        cost_estimate=FREE,
+        name="project",
+    )(order, *pieces, w_out, x)
+
+
 def eliminate(block):
     size = block.shape[0]
     row = lax.broadcasted_iota(jnp.int32, (size, size), 0)
     lane = lax.broadcasted_iota(jnp.int32, (size, size), 1)
-    both = jnp.concatenate([block, (row == lane).astype(F32)], axis=1)
-    tiles = [both[8 * i : 8 * i + 8, :] for i in range(size // 8)]
-    inside = lax.broadcasted_iota(jnp.int32, (8, 1), 0)
-    for j in range(size):
-        at, off = divmod(j, 8)
-        pivot = tiles[at][off : off + 1, :]
-        inverse = 1.0 / pivot[:, j : j + 1]
-        for i in range(at, size // 8):
-            if i == at and off == 7:
-                continue
-            share = tiles[i][:, j : j + 1] * inverse
-            if i == at:
-                share = jnp.where(inside > off, share, 0.0)
-            tiles[i] = tiles[i] - share * pivot
-    both = jnp.concatenate(tiles, axis=0)
-    diagonal = jnp.sum(jnp.where(row == lane, both[:, :size], 0.0), axis=1, keepdims=True)
-    return both[:, size:] * lax.rsqrt(diagonal)
+    unit = (row == lane).astype(F32)
+    left = [block[8 * i : 8 * i + 8, :] for i in range(size // 8)]
+    right = [unit[8 * i : 8 * i + 8, :] for i in range(size // 8)]
+    inside = lax.broadcasted_iota(jnp.int32, (8, size), 0)
+    wide = lambda tile, j: jnp.broadcast_to(tile[:, j : j + 1], (8, size))
+    for at in range(size // 8):
+        a, v = left[at], right[at]
+        cols = [wide(a, 8 * at + k) for k in range(8)]
+        inverses = []
+        for k in range(8):
+            inverse = 1.0 / cols[k][k : k + 1, :]
+            inverses.append(inverse)
+            share = jnp.where(inside > k, cols[k] * inverse, 0.0)
+            for l in range(k + 1, 8):
+                cols[l] = cols[l] - share * cols[l][k : k + 1, :]
+            a = a - share * a[k : k + 1, :]
+            v = v - share * v[k : k + 1, :]
+        left[at], right[at] = a, v
+        for i in range(at + 1, size // 8):
+            mine = [wide(left[i], 8 * at + k) for k in range(8)]
+            p, q = left[i], right[i]
+            for k in range(8):
+                share = mine[k] * inverses[k]
+                for l in range(k + 1, 8):
+                    mine[l] = mine[l] - share * cols[l][k : k + 1, :]
+                p = p - share * a[k : k + 1, :]
+                q = q - share * v[k : k + 1, :]
+            left[i], right[i] = p, q
+    upper = jnp.concatenate(left, axis=0)
+    diagonal = jnp.sum(jnp.where(row == lane, upper, 0.0), axis=1, keepdims=True)
+    return jnp.concatenate(right, axis=0) * lax.rsqrt(diagonal)
 
 
 def dot_high(a, b, contract):
@@ -310,7 +358,7 @@
     )(gram)
 
 
-def per_device(ids, embed, gain, w_in, feat_filter, inner_filter, w_out, cotangent, right_prev):
+def general_device(ids, embed, gain, w_in, feat_filter, inner_filter, w_out, cotangent, right_prev):
     size = lax.axis_size("fsdp")
     count = lax.axis_size("dp")
     tokens = ids[0]
@@ -391,6 +439,309 @@
     return (block_out, filter_grad, basis, right_factor)
 
 
+def finish_kernel(flag, *refs):
+    count = len(RELATIVE)
+    pieces = refs[:count]
+    side_own, side_other, cot_own, cot_other = refs[count : count + 4]
+    basis, right_raw, sums = refs[count + 4 : count + 7]
+    rows, cots, sides, inverse = refs[count + 7 :]
+    mine = flag[0]
+    other = 1 - mine
+    length = cots.shape[1]
+    local = pieces[0].shape[1]
+    for at, piece in enumerate(pieces):
+        lanes = slice(at * local, (at + 1) * local)
+        rows[mine, :, lanes] = piece[:length, :]
+        rows[other, :, lanes] = piece[length:, :]
+    sides[mine] = side_own[...]
+    sides[other] = side_other[...]
+    cots[mine] = cot_own[...]
+    cots[other] = cot_other[...]
+    turned = [sides[0], sides[1]]
+    first, second = rows[0], rows[1]
+    transposed = ((1,), (1,))
+    plain = ((1,), (0,))
+    soft = lambda a, b, contract: lax.dot_general(a, b, (contract, ((), ())), preferred_element_type=F32)
+    corner = soft(first, first, transposed)
+    across = soft(first, second, transposed)
+    across_t = soft(second, first, transposed)
+    end = soft(second, second, transposed)
+    upper = dot_high(corner, turned[0], plain) + dot_high(across, turned[1], plain)
+    under = dot_high(across_t, turned[0], plain) + dot_high(end, turned[1], plain)
+    rowwise = ((0,), (0,))
+    gram = dot_high(turned[0], upper, rowwise) + dot_high(turned[1], under, rowwise)
+    factor_kernel(gram, inverse)
+    scaled = inverse[...] * math.sqrt(local * count)
+    panel = jnp.zeros((local, gram.shape[0]), F32)
+    for i in (0, 1):
+        own = jnp.where(mine == i, pieces[0][:length, :], pieces[0][length:, :])
+        top = turned[i].astype(BF16)
+        rest = (turned[i] - top.astype(F32)).astype(BF16)
+        panel = panel + soft(own, top, rowwise) + soft(own, rest, rowwise)
+    basis[...] = dot_high(panel, scaled, transposed).astype(BF16)
+    raw = jnp.zeros(right_raw.shape, F32)
+    for i, product in enumerate((upper, under)):
+        turn = dot_high(product, scaled, transposed)
+        top = turn.astype(BF16)
+        rest = (turn - top.astype(F32)).astype(BF16)
+        raw = raw + soft(cots[i], top, ((0,), (0,))) + soft(cots[i], rest, ((0,), (0,)))
+    right_raw[...] = raw
+    sums[...] = jnp.sum(raw * raw, axis=0, keepdims=True)
+
+
+def finish(flag, pieces, side_own, side_other, cot_own, cot_other):
+    local = pieces[0].shape[1]
+    length, width = cot_own.shape
+    rank = side_own.shape[1]
+    count = len(pieces)
+    whole = pl.BlockSpec(memory_space=pltpu.VMEM)
+    return pl.pallas_call(
+        finish_kernel,
+        out_shape=(
+            jax.ShapeDtypeStruct((local, rank), BF16),
+            jax.ShapeDtypeStruct((width, rank), F32),
+            jax.ShapeDtypeStruct((1, rank), F32),
+        ),
+        in_specs=[pl.BlockSpec(memory_space=pltpu.SMEM)] + [whole] * (count + 4),
+        out_specs=(whole, whole, whole),
+        scratch_shapes=[
+            pltpu.VMEM((2, length, count * local), BF16),
+            pltpu.VMEM((2, length, width), BF16),
+            pltpu.VMEM((2, length, rank), F32),
+            pltpu.VMEM((rank, rank), F32),
+        ],
+        compiler_params=pltpu.CompilerParams(vmem_limit_bytes=20 * 2**20),
+        cost_estimate=pl.CostEstimate(flops=2**33, transcendentals=0, bytes_accessed=2**22),
+        name="finish",
+    )(flag, *pieces, side_own, side_other, cot_own, cot_other)
+
+
+FREE = pl.CostEstimate(flops=1, transcendentals=0, bytes_accessed=1)
+
+
+def copies_in(source, target, sems):
+    count = sems.shape[0]
+    rows = source.shape[0] // count
+    copies = []
+    for i in range(count):
+        part = pl.ds(i * rows, rows)
+        copies.append(pltpu.make_async_copy(source.at[part], target.at[part], sems.at[i]))
+        copies[-1].start()
+    return copies
+
+
+def parts_kernel(order, weights, cot, send, keep, here, sems, *, local):
+    half = send.shape[0]
+    for copy in copies_in(weights, here, sems):
+        copy.wait()
+    for slot in range(2 * half):
+        out, at = (send, slot) if slot < half else (keep, slot - half)
+        rows = here[pl.ds(pl.multiple_of(order[slot] * local, local), local), :]
+        out[at] = lax.dot_general(
+            cot[...], rows, (((1,), (1,)), ((), ())), preferred_element_type=F32
+        ).astype(BF16)
+
+
+def grad_parts(order, w_out, cot, size):
+    length = cot.shape[0]
+    local, half = w_out.shape[0] // size, size // 2
+    shape = jax.ShapeDtypeStruct((half, length, local), BF16)
+    whole = pl.BlockSpec(memory_space=pltpu.VMEM)
+    return pl.pallas_call(
+        functools.partial(parts_kernel, local=local),
+        out_shape=(shape, shape),
+        in_specs=[pl.BlockSpec(memory_space=pltpu.SMEM), pl.BlockSpec(memory_space=pltpu.HBM), whole],
+        out_specs=(whole, whole),
+        scratch_shapes=[pltpu.VMEM(w_out.shape, w_out.dtype), pltpu.SemaphoreType.DMA((8,))],
+        compiler_params=pltpu.CompilerParams(vmem_limit_bytes=16 * 2**20),
+        cost_estimate=FREE,
+        name="grad_parts",
+    )(order, w_out, cot)
+
+
+RELATIVE = (0, 2, 4, 6, 8, 10, 12, 14, 1, 3, 5, 7, 9, 11, 13, 15)
+
+
+def mix_whole_kernel(order, *refs, length):
+    count = len(RELATIVE)
+    pieces, weights = refs[:count], refs[count]
+    feat, inner = refs[count + 1 : count + 3]
+    y_out, qkv_out, saved = refs[count + 3 : count + 6]
+    normed, pad, here, sems = refs[count + 6 :]
+    copies = [copies_in(weights.at[i], here.at[i], sems.at[i]) for i in range(3)]
+    taps = inner.shape[0]
+    step = pieces[0].shape[1]
+    squares = jnp.zeros((length, step), F32)
+    for piece in pieces:
+        a = piece[:length, :].astype(F32)
+        squares = squares + a * a
+    scale = lax.rsqrt(jnp.sum(squares, axis=1, keepdims=True) / (step * count) + 1e-05)
+    for slot, piece in enumerate(pieces):
+        place = pl.ds(pl.multiple_of(order[slot] * step, step), step)
+        gain = piece[length:, :][0:1].astype(F32)
+        normed[:, place] = (piece[:length, :].astype(F32) * scale * gain).astype(BF16)
+    convs = []
+    for which in range(3):
+        for copy in copies[which]:
+            copy.wait()
+        half = lax.dot_general(
+            normed[...], here[which], (((1,), (1,)), ((), ())), preferred_element_type=F32
+        ).astype(BF16)
+        qkv_out[which] = half
+        pad_front(pad, half.astype(F32))
+        result = jnp.zeros(half.shape, F32)
+        for lag in range(taps):
+            result = result + feat[which, lag : lag + 1, :] * lagged(pad, lag, length)
+        convs.append(result)
+        saved[which] = result
+    gated = convs[1] * convs[2]
+    saved[3] = gated
+    pad_front(pad, gated)
+    window = jnp.zeros(gated.shape, F32)
+    for lag in range(taps):
+        window = window + inner[lag : lag + 1, :] * lagged(pad, lag, length)
+    saved[4] = window
+    y_out[...] = (convs[0] * window).astype(BF16)
+
+
+def mix_whole(order, pieces, w_in, feat, inner):
+    rows, step = pieces[0].shape
+    length = rows - EXTRA
+    local, width = w_in.shape[1:]
+    whole = pl.BlockSpec(memory_space=pltpu.VMEM)
+    return pl.pallas_call(
+        functools.partial(mix_whole_kernel, length=length),
+        out_shape=(
+            jax.ShapeDtypeStruct((length, local), BF16),
+            jax.ShapeDtypeStruct((3, length, local), BF16),
+            jax.ShapeDtypeStruct((5, length, local), F32),
+        ),
+        in_specs=[pl.BlockSpec(memory_space=pltpu.SMEM)]
+        + [whole] * len(pieces)
+        + [pl.BlockSpec(memory_space=pltpu.HBM), whole, whole],
+        out_specs=(whole, whole, whole),
+        scratch_shapes=[
+            pltpu.VMEM((length, width), BF16),
+            pltpu.VMEM((length + 16, local), F32),
+            pltpu.VMEM(w_in.shape, w_in.dtype),
+            pltpu.SemaphoreType.DMA((3, 4)),
+        ],
+        compiler_params=pltpu.CompilerParams(vmem_limit_bytes=24 * 2**20),
+        cost_estimate=pl.CostEstimate(
+            flops=6 * length * local * width, transcendentals=0, bytes_accessed=6 * local * width
+        ),
+        name="mix",
+    )(order, *pieces, w_in, feat, inner)
+
+
+def after(value, *events):
+    return lax.optimization_barrier((value,) + events)[0]
+
+
+def terms_kernel(summed, qkv, saved, inner, pool, out, pad, stack, sums, *, scale):
+    taps_kernel(summed, qkv, saved, inner, pool, sums, pad, stack)
+    out[...] = (sums[...] * scale).astype(BF16)
+
+
+def filter_terms(summed, qkv, saved, inner, groups, scale):
+    length, local = qkv.shape[1:]
+    member = jnp.arange(local)[:, None] // (local // groups) == jnp.arange(groups)[None, :]
+    return pl.pallas_call(
+        functools.partial(terms_kernel, scale=scale),
+        out_shape=jax.ShapeDtypeStruct((32, groups), BF16),
+        scratch_shapes=[
+            pltpu.VMEM((length + 16, local), F32),
+            pltpu.VMEM((32, local), F32),
+            pltpu.VMEM((32, groups), F32),
+        ],
+        cost_estimate=FREE,
+        name="filter_terms",
+    )(summed, qkv, saved, inner, member.astype(F32))
+
+
+def hop_all(piece, size):
+    send = functools.partial(exchange, axis="fsdp", size=size)
+    have = {0: piece}
+    for z in (4, 8, 12):
+        have[z] = send(piece, bits=z)
+    for z in (0, 4, 8, 12):
+        have[z + 2] = send(have[z], bits=2)
+    for near in (0, 4, 2, 6, 8, 10, 12, 14):
+        have[near + 1] = send(have[near], bits=1)
+    return have
+
+
+def both_ways(value, bits, size):
+    half = value.astype(BF16)
+    return half.astype(F32) + exchange(half, "fsdp", size, bits).astype(F32)
+
+
+def tuned_device(ids, embed, gain, w_in, feat_filter, inner_filter, w_out, cotangent, right_prev):
+    size = lax.axis_size("fsdp")
+    count = lax.axis_size("dp")
+    tokens = ids[0]
+    length = tokens.shape[0]
+    vocab, width = embed.shape
+    local = w_in.shape[1]
+    rank = right_prev.shape[1]
+    index = lax.axis_index("fsdp").astype(jnp.int32)
+    order = jnp.bitwise_xor(index, jnp.array(RELATIVE, jnp.int32))
+    flag = lax.axis_index("dp").astype(jnp.int32)[None]
+    send = functools.partial(exchange, axis="fsdp", size=size)
+    feat = spread(feat_filter, local)
+    inner = spread(inner_filter, local)
+
+    onehot = (tokens[:, None] == jnp.arange(vocab, dtype=jnp.int32)[None, :]).astype(BF16)
+    x_cols = jnp.dot(onehot, embed, preferred_element_type=F32).astype(BF16)
+    x_sent = jnp.concatenate([x_cols, jnp.broadcast_to(gain[None, :], (EXTRA, width))], axis=0)
+    have = hop_all(x_sent, size)
+    w_in = pltpu.with_memory_space_constraint(w_in, pltpu.HBM)
+    w_out = pltpu.with_memory_space_constraint(w_out, pltpu.HBM)
+
+    cot_cols = cotangent[0]
+    turns = [c + x + f + n for c in (1, 0) for x in (2, 0) for f in (8, 0) for n in (4, 0)]
+    targets = jnp.bitwise_xor(index, jnp.array(turns, jnp.int32))
+    away, keep = grad_parts(targets, w_out, cot_cols, size)
+    keep = keep.astype(F32) + send(away, bits=1).astype(F32)
+    away, keep = keep[:4].astype(BF16), keep[4:]
+    keep = keep + send(away, bits=2).astype(F32)
+    away, keep = keep[:2].astype(BF16), keep[2:]
+    side = jnp.dot(cot_cols, right_prev, preferred_element_type=F32)
+    side = both_ways(side, 1, size)
+    ready = after(order, side, away, keep)
+    y, qkv, saved = mix_whole(ready, [have[r] for r in RELATIVE], w_in, feat, inner)
+
+    keep = keep + send(away, bits=8).astype(F32)
+    y_grad = (keep[1:] + send(keep[:1].astype(BF16), bits=4).astype(F32))[0]
+    for bits in (2, 4, 8):
+        side = both_ways(side, bits, size)
+    side_other = exchange(side, "dp", count, 1)
+
+    y_other = exchange(y, "dp", count, 1)
+    got = hop_all(jnp.concatenate([y, y_other], axis=0), size)
+    cot_other = exchange(after(cot_cols, got[4]), "dp", count, 1)
+    groups = feat_filter.shape[1]
+    scale = 1.0 / math.sqrt(count * length)
+    terms = filter_terms(after(y_grad, got[12]), qkv, saved, inner, groups, scale)
+    terms_other = exchange(terms, "dp", count, 1)
+    filter_grad = terms.astype(F32) + terms_other.astype(F32)
+    filter_grad = jnp.swapaxes(filter_grad.reshape(4, 8, groups), 1, 2)[:, :, : inner.shape[0]]
+    got[15] = send(after(got[14], terms), bits=1)
+    pieces = [got[r] for r in RELATIVE]
+    basis, right_raw, sums = finish(flag, pieces, side, side_other, cot_cols, cot_other)
+    column_sums = plane_sum(sums, size)
+    block_out = project_whole(order, pieces, w_out, x_sent)[None]
+    right_factor = right_raw * lax.rsqrt(column_sums / (size * width) + 1e-06)
+    return (block_out, filter_grad, basis, right_factor)
+
+
+def per_device(ids, embed, gain, w_in, feat_filter, inner_filter, w_out, cotangent, right_prev):
+    sizes = (lax.axis_size("dp"), lax.axis_size("fsdp"))
+    shapes = (ids.shape[1], w_in.shape[1], right_prev.shape[1])
+    body = tuned_device if sizes == (2, 16) and shapes == (192, 256, 256) else general_device
+    return body(ids, embed, gain, w_in, feat_filter, inner_filter, w_out, cotangent, right_prev)
+
+
 def solution(mesh):
     placed = (
         P("dp", None),

time: 174 us -> 135 us (0.78)
  matrix products: 14.4 us -> 0.52 us
  other arithmetic: 13.2 us -> 4.59 us
  local copies, waits for them, and re-layouts: 12.8 us -> 4.67 us
  Pallas kernels: 43.2 us -> 38.5 us
  starting transfers between devices: 46.6 us -> 44.4 us
    dot_general x10 -> x2, matrix products: 14.4 us -> 0.52 us  [the longest x1 0.31 us: tuned_device(): x_cols = jnp.dot(onehot, embed, preferred_element_type=F32).astype(BF16)]
    pallas_call x4 -> x5, Pallas kernels: 43.2 us -> 38.5 us  [the longest x1 15.6 us: finish(): pl.pallas_call(finish_kernel, out_shape=(jax.ShapeDtypeStruct((local, ran...]
    squeeze x4 -> x1, other arithmetic: 3.81 us -> 0.7 us  [tuned_device(): y_grad = (keep[1:] + send(keep[:1].astype(BF16), bits=4).astype(F32))[0]]
    ppermute x36 -> x46, starting transfers between devices: 46.6 us -> 44.4 us  [exchange(): return lax.ppermute(value, axis, [(i, i ^ bits) for i in range(size)])]
    gather x2 -> x0, local copies, waits for them, and re-layouts: 1.83 us -> none  [per_device(): pieces.append(part[slots].reshape(rank, local)[:, :length].T)]
    transpose x2 -> x0, local copies, waits for them, and re-layouts: 1.81 us -> none  [the longest x1 1.78 us: per_device(): flat = stacked.transpose(0, 2, 1, 3).reshape(count * length, size * local)]
    ppermute x36 -> x46, waiting for transfers between devices: 42 us -> 40.9 us  [exchange(): return lax.ppermute(value, axis, [(i, i ^ bits) for i in range(size)])]
    unnamed x48 -> x31, local copies, waits for them, and re-layouts: 3.52 us -> 3.58 us
  transfers between devices with their start and end apart: 36 -> 46, of which waited for: 12 -> 18; matrix products, arithmetic and copies ran while one was open for 7% -> 3% of each run, Pallas kernels for 9% -> 14%
where the time goes in v2:
time: 135 us
  starting transfers between devices  44.4 us (33%)
  waiting for transfers between devices  40.9 us (30%)
  Pallas kernels  38.5 us (29%)
  local copies, waits for them, and re-layouts  4.67 us (3%)
  other arithmetic  4.59 us (3%)
    ppermute x46, starting transfers between devices, exchange(): return lax.ppermute(value, axis, [(i, i ^ bits) for i in range(size)])  44.4 us
    ppermute x46, waiting for transfers between devices, exchange(): return lax.ppermute(value, axis, [(i, i ^ bits) for i in range(size)])  40.9 us
    pallas_call x1, Pallas kernels, finish(): pl.pallas_call(finish_kernel, out_shape=(jax.ShapeDtypeStruct((local, ran...  15.6 us
    pallas_call x1, Pallas kernels, mix_whole(): pl.pallas_call(functools.partial(mix_whole_kernel, length=length), out_sh...  10 us
    pallas_call x1, Pallas kernels, project_whole(): pl.pallas_call(functools.partial(out_whole_kernel, length=length, local=l...  5.1 us
    pallas_call x1, Pallas kernels, grad_parts(): pl.pallas_call(functools.partial(parts_kernel, local=local), out_shape=(s...  4.3 us
    unnamed x31, local copies, waits for them, and re-layouts  3.58 us
    pallas_call x1, Pallas kernels, filter_terms(): pl.pallas_call(functools.partial(terms_kernel, scale=scale), out_shape=ja...  3.5 us
  transfers between devices with their start and end apart: 46, of which 18 were waited for; matrix products, arithmetic and copies ran while one was open for 3% of the time, Pallas kernels for 14%

profile of v2, /device:TPU:0, one launch (start us, length us, event | category | flops | bytes accessed | tf_op | source)
XLA Modules:
  0.0 134.5 jit_solution(12416008197142389912)
XLA Ops:
  2.3 4.3 %grad_parts.1 = (bf16[8,192,256]{2,1,0:T(8,128)(2,1)S(1)}, bf16[8,192,256]{2,1,0:T(8,128)(2,1)S(1)}) custom-call(s32[16]{0:T(128)S(1)} %broadcast_xor_fusion.order, bf16[4096,512]{1,0:T(8,128)(2,1)} %refs_16_.3, bf16[192,512]{1,0:T(8,128)(2,1)S(1)} %bitcast.20), custom_call_target="tpu_custom_call" | custom-call | flops 1 | bytes 1 | tf_op jit(solution)/shard_map/grad_parts/pallas_call | solution.py:550
  7.9 3.1 %collective-permute-start.4 = (bf16[208,512]{1,0:T(8,128)(2,1)S(1)}, bf16[208,512]{1,0:T(8,128)(2,1)S(1)}, u32[]{:S(2)}, u32[]{:S(2)}) collective-permute-start(bf16[208,512]{1,0:T(8,128)(2,1)S(1)} %pad_maximum_fusion.refs_0_.refs_17_), channel_id=1, source_target_pairs={{0,4},{1,5},{2,6},{3,7},{4,0},{5,1},{6,2},{7,3},{8,12},{9,13},{10,... | collective-permute-start | bytes 638984 | tf_op jit(solution)/shard_map/ppermute | solution.py:18
  10.9 2.6 %collective-permute-start.6 = (bf16[208,512]{1,0:T(8,128)(2,1)S(1)}, bf16[208,512]{1,0:T(8,128)(2,1)S(1)}, u32[]{:S(2)}, u32[]{:S(2)}) collective-permute-start(bf16[208,512]{1,0:T(8,128)(2,1)S(1)} %pad_maximum_fusion.refs_0_.refs_17_), channel_id=1, source_target_pairs={{0,8},{1,9},{2,10},{3,11},{4,12},{5,13},{6,14},{7,15},{8,0},{9,1},... | collective-permute-start | bytes 638984 | tf_op jit(solution)/shard_map/ppermute | solution.py:18
  13.6 1.8 %collective-permute-start.37 = (bf16[192,256]{1,0:T(8,128)(2,1)S(1)}, bf16[192,256]{1,0:T(8,128)(2,1)S(1)}, u32[]{:S(2)}, u32[]{:S(2)}) collective-permute-start(bf16[192,256]{1,0:T(8,128)(2,1)S(1)} %fusion.4), channel_id=1, source_target_pairs={{0,2},{1,3},{2,0},{3,1},{4,6},{5,7},{6,4},{7,5},{8,10},{9,11},{10,... | collective-permute-start | bytes 294920 | tf_op jit(solution)/shard_map/ppermute | solution.py:18
  15.8 2.5 %collective-permute-done.37 = bf16[192,256]{1,0:T(8,128)(2,1)S(1)} collective-permute-done((bf16[192,256]{1,0:T(8,128)(2,1)S(1)}, bf16[192,256]{1,0:T(8,128)(2,1)S(1)}, u32[]{:S(2)}, u32[]{:S(2)}) %collective-permute-start.37) | collective-permute-done | bytes 98336 | tf_op jit(solution)/shard_map/ppermute | solution.py:18
  18.3 1.7 %collective-permute-start.3 = (bf16[208,512]{1,0:T(8,128)(2,1)S(1)}, bf16[208,512]{1,0:T(8,128)(2,1)S(1)}, u32[]{:S(2)}, u32[]{:S(2)}) collective-permute-start(bf16[208,512]{1,0:T(8,128)(2,1)S(1)} %pad_maximum_fusion.refs_0_.refs_17_), channel_id=1, source_target_pairs={{0,2},{1,3},{2,0},{3,1},{4,6},{5,7},{6,4},{7,5},{8,10},{9,11},{10,... | collective-permute-start | bytes 638984 | tf_op jit(solution)/shard_map/ppermute | solution.py:18
  22.2 7.0 %collective-permute-done.6.refs_4_ = bf16[208,512]{1,0:T(8,128)(2,1)S(1)} collective-permute-done((bf16[208,512]{1,0:T(8,128)(2,1)S(1)}, bf16[208,512]{1,0:T(8,128)(2,1)S(1)}, u32[]{:S(2)}, u32[]{:S(2)}) %collective-permute-start.6) | collective-permute-done | bytes 213024 | tf_op jit(solution)/shard_map/ppermute | solution.py:18
  31.2 2.9 %collective-permute-start.39 = (bf16[192,256]{1,0:T(8,128)(2,1)S(1)}, bf16[192,256]{1,0:T(8,128)(2,1)S(1)}, u32[]{:S(2)}, u32[]{:S(2)}) collective-permute-start(bf16[192,256]{1,0:T(8,128)(2,1)S(1)} %add_convert_fusion), channel_id=1, source_target_pairs={{0,8},{1,9},{2,10},{3,11},{4,12},{5,13},{6,14},{7,15},{8,0},{9,1},... | collective-permute-start | bytes 294920 | tf_op jit(solution)/shard_map/ppermute | solution.py:18
  38.6 7.6 %collective-permute-done.7.refs_5_ = bf16[208,512]{1,0:T(8,128)(2,1)S(1)} collective-permute-done((bf16[208,512]{1,0:T(8,128)(2,1)S(1)}, bf16[208,512]{1,0:T(8,128)(2,1)S(1)}, u32[]{:S(2)}, u32[]{:S(2)}) %collective-permute-start.7) | collective-permute-done | bytes 213024 | tf_op jit(solution)/shard_map/ppermute | solution.py:18
  46.2 2.4 %collective-permute-done.9.refs_7_ = bf16[208,512]{1,0:T(8,128)(2,1)S(1)} collective-permute-done((bf16[208,512]{1,0:T(8,128)(2,1)S(1)}, bf16[208,512]{1,0:T(8,128)(2,1)S(1)}, u32[]{:S(2)}, u32[]{:S(2)}) %collective-permute-start.9) | collective-permute-done | bytes 213024 | tf_op jit(solution)/shard_map/ppermute | solution.py:18
  51.4 3.4 %collective-permute-start.33 = (bf16[2,192,256]{2,1,0:T(8,128)(2,1)S(1)}, bf16[2,192,256]{2,1,0:T(8,128)(2,1)S(1)}, u32[]{:S(2)}, u32[]{:S(2)}) collective-permute-start(bf16[2,192,256]{2,1,0:T(8,128)(2,1)S(1)} %slice.47), channel_id=1, source_target_pairs={{0,8},{1,9},{2,10},{3,11},{4,12},{5,13},{6,14},{7,15},{8,0},{9,1},... | collective-permute-start | bytes 589832 | tf_op jit(solution)/shard_map/ppermute | solution.py:18
  54.8 10.0 %mix.1 = (bf16[192,256]{1,0:T(8,128)(2,1)S(1)}, bf16[3,192,256]{2,1,0:T(8,128)(2,1)S(1)}, f32[5,192,256]{2,1,0:T(8,128)S(1)}) custom-call(s32[16]{0:T(128)S(1)} %broadcast_xor_fusion.1.order, bf16[208,512]{1,0:T(8,128)(2,1)S(1)} %pad_maximum_fusion.refs_0_.refs_17_, bf16[208,512]{1,0:T(8,128)(2,1)S(1)} %collective-permute-done.3.refs_1_, ...), custom_call_target="tpu_custom_call" | custom-call | flops 2415919104 | bytes 12582912 | tf_op jit(solution)/shard_map/mix/pallas_call | solution.py:612
  66.3 4.1 %collective-permute-done.18 = bf16[192,256]{1,0:T(8,128)(2,1)S(1)} collective-permute-done((bf16[192,256]{1,0:T(8,128)(2,1)S(1)}, bf16[192,256]{1,0:T(8,128)(2,1)S(1)}, u32[]{:S(2)}, u32[]{:S(2)}) %collective-permute-start.18) | collective-permute-done | bytes 98336 | tf_op jit(solution)/shard_map/ppermute | solution.py:18
  72.4 2.5 %collective-permute-start.22 = (bf16[384,256]{1,0:T(8,128)(2,1)S(1)}, bf16[384,256]{1,0:T(8,128)(2,1)S(1)}, u32[]{:S(2)}, u32[]{:S(2)}) collective-permute-start(bf16[384,256]{1,0:T(8,128)(2,1)S(1)} %constant_dynamic-update-slice_fusion.refs_0_), channel_id=1, source_target_pairs={{0,8},{1,9},{2,10},{3,11},{4,12},{5,13},{6,14},{7,15},{8,0},{9,1},... | collective-permute-start | bytes 589832 | tf_op jit(solution)/shard_map/ppermute | solution.py:18
  77.1 3.1 %collective-permute-done.24.refs_6_ = bf16[384,256]{1,0:T(8,128)(2,1)S(1)} collective-permute-done((bf16[384,256]{1,0:T(8,128)(2,1)S(1)}, bf16[384,256]{1,0:T(8,128)(2,1)S(1)}, u32[]{:S(2)}, u32[]{:S(2)}) %collective-permute-start.24) | collective-permute-done | bytes 196640 | tf_op jit(solution)/shard_map/ppermute | solution.py:18
  80.2 4.3 %collective-permute-start.34 = (bf16[1,192,256]{2,1,0:T(8,128)(2,1)S(1)}, bf16[1,192,256]{2,1,0:T(8,128)(2,1)S(1)}, u32[]{:S(2)}, u32[]{:S(2)}) collective-permute-start(bf16[1,192,256]{2,1,0:T(8,128)(2,1)S(1)} %slice.48), channel_id=1, source_target_pairs={{0,4},{1,5},{2,6},{3,7},{4,0},{5,1},{6,2},{7,3},{8,12},{9,13},{10,... | collective-permute-start | bytes 294920 | tf_op jit(solution)/shard_map/ppermute | solution.py:18
  87.6 1.9 %collective-permute-done.22.refs_4_ = bf16[384,256]{1,0:T(8,128)(2,1)S(1)} collective-permute-done((bf16[384,256]{1,0:T(8,128)(2,1)S(1)}, bf16[384,256]{1,0:T(8,128)(2,1)S(1)}, u32[]{:S(2)}, u32[]{:S(2)}) %collective-permute-start.22) | collective-permute-done | bytes 196640 | tf_op jit(solution)/shard_map/ppermute | solution.py:18
  92.5 3.5 %filter_terms.1 = bf16[32,16]{1,0:T(8,128)(2,1)} custom-call(f32[192,256]{1,0:T(8,128)} %fusion.summed, bf16[3,192,256]{2,1,0:T(8,128)(2,1)} %copy-done.4, f32[5,192,256]{2,1,0:T(8,128)} %copy-done.1, f32[7,256]{1,0:T(8,128)} %copy-done.5, f32[256,16]{1,0:T(8,128)} %fusion.2.pool), custom_call_target="tpu_custom_call" | custom-call | flops 1 | bytes 1 | tf_op jit(solution)/shard_map/filter_terms/pallas_call | solution.py:649
  97.2 2.7 %collective-permute-done.23.refs_5_ = bf16[384,256]{1,0:T(8,128)(2,1)S(1)} collective-permute-done((bf16[384,256]{1,0:T(8,128)(2,1)S(1)}, bf16[384,256]{1,0:T(8,128)(2,1)S(1)}, u32[]{:S(2)}, u32[]{:S(2)}) %collective-permute-start.23) | collective-permute-done | bytes 196640 | tf_op jit(solution)/shard_map/ppermute | solution.py:18
  103.3 15.6 %finish.1 = (bf16[256,256]{1,0:T(8,128)(2,1)}, f32[512,256]{1,0:T(8,128)S(1)}, f32[1,256]{1,0:T(1,128)S(1)}) custom-call(s32[1]{0:T(128)} %bitcast.8.flag, bf16[384,256]{1,0:T(8,128)(2,1)S(1)} %constant_dynamic-update-slice_fusion.refs_0_, bf16[384,256]{1,0:T(8,128)(2,1)S(1)} %collective-permute-done.19.refs_1_, ...), custom_call_target="tpu_custom_call" | custom-call | flops 8589934592 | bytes 4194304 | tf_op jit(solution)/shard_map/finish/pallas_call | solution.py:498
  120.1 1.6 %collective-permute-start.43 = (f32[1,256]{1,0:T(1,128)S(1)}, f32[1,256]{1,0:T(1,128)S(1)}, u32[]{:S(2)}, u32[]{:S(2)}) collective-permute-start(f32[1,256]{1,0:T(1,128)S(1)} %add.60), channel_id=1, source_target_pairs={{0,2},{1,3},{2,0},{3,1},{4,6},{5,7},{6,4},{7,5},{8,10},{9,11},{10,... | collective-permute-start | bytes 3080 | tf_op jit(solution)/shard_map/ppermute | solution.py:18
  121.7 1.9 %collective-permute-done.43 = f32[1,256]{1,0:T(1,128)S(1)} collective-permute-done((f32[1,256]{1,0:T(1,128)S(1)}, f32[1,256]{1,0:T(1,128)S(1)}, u32[]{:S(2)}, u32[]{:S(2)}) %collective-permute-start.43) | collective-permute-done | bytes 1056 | tf_op jit(solution)/shard_map/ppermute | solution.py:18
  124.7 2.5 %collective-permute-done.44 = f32[1,256]{1,0:T(1,128)S(1)} collective-permute-done((f32[1,256]{1,0:T(1,128)S(1)}, f32[1,256]{1,0:T(1,128)S(1)}, u32[]{:S(2)}, u32[]{:S(2)}) %collective-permute-start.44) | collective-permute-done | bytes 1056 | tf_op jit(solution)/shard_map/ppermute | solution.py:18
  128.6 5.1 %project.1 = bf16[192,512]{1,0:T(8,128)(2,1)} custom-call(s32[16]{0:T(128)S(1)} %broadcast_xor_fusion.1.order, bf16[384,256]{1,0:T(8,128)(2,1)S(1)} %constant_dynamic-update-slice_fusion.refs_0_, bf16[384,256]{1,0:T(8,128)(2,1)S(1)} %collective-permute-done.19.refs_1_, bf16[384,256]{1,0:T(8,128)(2,1)S(1)} %collective-permute-done.20.refs_2_, ...), custom_call_target="tpu_custom_call" | custom-call | flops 1 | bytes 1 | tf_op jit(solution)/shard_map/project/pallas_call | solution.py:285
  (136 shorter events, 35.7 us)
Async XLA Ops:
  6.6 13.4 %collective-permute-start.1 = (bf16[8,192,256]{2,1,0:T(8,128)(2,1)S(1)}, bf16[8,192,256]{2,1,0:T(8,128)(2,1)}, u32[]{:S(2)}, u32[]{:S(2)}) collective-permute-start(bf16[8,192,256]{2,1,0:T(8,128)(2,1)S(1)} %get-tuple-element.17), channel_id=1, source_target_pairs={{0,1},{1,0},{2,3},{3,2},{4,5},{5,4},{6,7},{7,6},{8,9},{9,8},{10,11... | collective-permute-start | bytes 2359304 | tf_op jit(solution)/shard_map/ppermute | solution.py:18
  7.9 14.3 %collective-permute-start.4 = (bf16[208,512]{1,0:T(8,128)(2,1)S(1)}, bf16[208,512]{1,0:T(8,128)(2,1)S(1)}, u32[]{:S(2)}, u32[]{:S(2)}) collective-permute-start(bf16[208,512]{1,0:T(8,128)(2,1)S(1)} %pad_maximum_fusion.refs_0_.refs_17_), channel_id=1, source_target_pairs={{0,4},{1,5},{2,6},{3,7},{4,0},{5,1},{6,2},{7,3},{8,12},{9,13},{10,... | collective-permute-start | bytes 638984 | tf_op jit(solution)/shard_map/ppermute | solution.py:18
  10.9 18.2 %collective-permute-start.6 = (bf16[208,512]{1,0:T(8,128)(2,1)S(1)}, bf16[208,512]{1,0:T(8,128)(2,1)S(1)}, u32[]{:S(2)}, u32[]{:S(2)}) collective-permute-start(bf16[208,512]{1,0:T(8,128)(2,1)S(1)} %pad_maximum_fusion.refs_0_.refs_17_), channel_id=1, source_target_pairs={{0,8},{1,9},{2,10},{3,11},{4,12},{5,13},{6,14},{7,15},{8,0},{9,1},... | collective-permute-start | bytes 638984 | tf_op jit(solution)/shard_map/ppermute | solution.py:18
  13.5 17.7 %collective-permute-start.8 = (bf16[208,512]{1,0:T(8,128)(2,1)S(1)}, bf16[208,512]{1,0:T(8,128)(2,1)S(1)}, u32[]{:S(2)}, u32[]{:S(2)}) collective-permute-start(bf16[208,512]{1,0:T(8,128)(2,1)S(1)} %pad_maximum_fusion.refs_0_.refs_17_), channel_id=1, source_target_pairs={{0,12},{1,13},{2,14},{3,15},{4,8},{5,9},{6,10},{7,11},{8,4},{9,5},... | collective-permute-start | bytes 638984 | tf_op jit(solution)/shard_map/ppermute | solution.py:18
  18.3 15.9 %collective-permute-start.3 = (bf16[208,512]{1,0:T(8,128)(2,1)S(1)}, bf16[208,512]{1,0:T(8,128)(2,1)S(1)}, u32[]{:S(2)}, u32[]{:S(2)}) collective-permute-start(bf16[208,512]{1,0:T(8,128)(2,1)S(1)} %pad_maximum_fusion.refs_0_.refs_17_), channel_id=1, source_target_pairs={{0,2},{1,3},{2,0},{3,1},{4,6},{5,7},{6,4},{7,5},{8,10},{9,11},{10,... | collective-permute-start | bytes 638984 | tf_op jit(solution)/shard_map/ppermute | solution.py:18
  20.0 10.7 %collective-permute-start.38 = (bf16[192,256]{1,0:T(8,128)(2,1)S(1)}, bf16[192,256]{1,0:T(8,128)(2,1)S(1)}, u32[]{:S(2)}, u32[]{:S(2)}) collective-permute-start(bf16[192,256]{1,0:T(8,128)(2,1)S(1)} %add_convert_fusion.1), channel_id=1, source_target_pairs={{0,4},{1,5},{2,6},{3,7},{4,0},{5,1},{6,2},{7,3},{8,12},{9,13},{10,... | collective-permute-start | bytes 294920 | tf_op jit(solution)/shard_map/ppermute | solution.py:18
  22.1 12.0 %collective-permute-start.10 = (bf16[208,512]{1,0:T(8,128)(2,1)S(1)}, bf16[208,512]{1,0:T(8,128)(2,1)S(1)}, u32[]{:S(2)}, u32[]{:S(2)}) collective-permute-start(bf16[208,512]{1,0:T(8,128)(2,1)S(1)} %pad_maximum_fusion.refs_0_.refs_17_), channel_id=1, source_target_pairs={{0,1},{1,0},{2,3},{3,2},{4,5},{5,4},{6,7},{7,6},{8,9},{9,8},{10,11... | collective-permute-start | bytes 638984 | tf_op jit(solution)/shard_map/ppermute | solution.py:18
  29.2 7.9 %collective-permute-start.5 = (bf16[208,512]{1,0:T(8,128)(2,1)S(1)}, bf16[208,512]{1,0:T(8,128)(2,1)S(1)}, u32[]{:S(2)}, u32[]{:S(2)}) collective-permute-start(bf16[208,512]{1,0:T(8,128)(2,1)S(1)} %collective-permute-done.4.refs_2_), channel_id=1, source_target_pairs={{0,2},{1,3},{2,0},{3,1},{4,6},{5,7},{6,4},{7,5},{8,10},{9,11},{10,... | collective-permute-start | bytes 638984 | tf_op jit(solution)/shard_map/ppermute | solution.py:18
  30.7 18.5 %collective-permute-start.2 = (bf16[4,192,256]{2,1,0:T(8,128)(2,1)S(1)}, bf16[4,192,256]{2,1,0:T(8,128)(2,1)S(1)}, u32[]{:S(2)}, u32[]{:S(2)}) collective-permute-start(bf16[4,192,256]{2,1,0:T(8,128)(2,1)S(1)} %slice.46), channel_id=1, source_target_pairs={{0,2},{1,3},{2,0},{3,1},{4,6},{5,7},{6,4},{7,5},{8,10},{9,11},{10,... | collective-permute-start | bytes 1179656 | tf_op jit(solution)/shard_map/ppermute | solution.py:18
  34.1 14.5 %collective-permute-start.12 = (bf16[208,512]{1,0:T(8,128)(2,1)S(1)}, bf16[208,512]{1,0:T(8,128)(2,1)S(1)}, u32[]{:S(2)}, u32[]{:S(2)}) collective-permute-start(bf16[208,512]{1,0:T(8,128)(2,1)S(1)} %collective-permute-done.4.refs_2_), channel_id=1, source_target_pairs={{0,1},{1,0},{2,3},{3,2},{4,5},{5,4},{6,7},{7,6},{8,9},{9,8},{10,11... | collective-permute-start | bytes 638984 | tf_op jit(solution)/shard_map/ppermute | solution.py:18
  34.1 12.1 %collective-permute-start.7 = (bf16[208,512]{1,0:T(8,128)(2,1)S(1)}, bf16[208,512]{1,0:T(8,128)(2,1)S(1)}, u32[]{:S(2)}, u32[]{:S(2)}) collective-permute-start(bf16[208,512]{1,0:T(8,128)(2,1)S(1)} %collective-permute-done.6.refs_4_), channel_id=1, source_target_pairs={{0,2},{1,3},{2,0},{3,1},{4,6},{5,7},{6,4},{7,5},{8,10},{9,11},{10,... | collective-permute-start | bytes 638984 | tf_op jit(solution)/shard_map/ppermute | solution.py:18
  37.1 12.0 %collective-permute-start.14 = (bf16[208,512]{1,0:T(8,128)(2,1)S(1)}, bf16[208,512]{1,0:T(8,128)(2,1)S(1)}, u32[]{:S(2)}, u32[]{:S(2)}) collective-permute-start(bf16[208,512]{1,0:T(8,128)(2,1)S(1)} %collective-permute-done.6.refs_4_), channel_id=1, source_target_pairs={{0,1},{1,0},{2,3},{3,2},{4,5},{5,4},{6,7},{7,6},{8,9},{9,8},{10,11... | collective-permute-start | bytes 638984 | tf_op jit(solution)/shard_map/ppermute | solution.py:18
  37.1 11.5 %collective-permute-start.9 = (bf16[208,512]{1,0:T(8,128)(2,1)S(1)}, bf16[208,512]{1,0:T(8,128)(2,1)S(1)}, u32[]{:S(2)}, u32[]{:S(2)}) collective-permute-start(bf16[208,512]{1,0:T(8,128)(2,1)S(1)} %collective-permute-done.8.refs_6_), channel_id=1, source_target_pairs={{0,2},{1,3},{2,0},{3,1},{4,6},{5,7},{6,4},{7,5},{8,10},{9,11},{10,... | collective-permute-start | bytes 638984 | tf_op jit(solution)/shard_map/ppermute | solution.py:18
  49.8 26.7 %collective-permute-start.40 = (f32[192,256]{1,0:T(8,128)S(1)}, f32[192,256]{1,0:T(8,128)S(1)}, u32[]{:S(2)}, u32[]{:S(2)}) collective-permute-start(f32[192,256]{1,0:T(8,128)S(1)} %convert_add_fusion.2.refs_16_), channel_id=1, source_target_pairs={{0,16},{16,0},{1,17},{17,1},{2,18},{18,2},{3,19},{19,3},{4,20},{20... | collective-permute-start | bytes 589832 | tf_op jit(solution)/shard_map/ppermute | solution.py:18
  51.4 23.5 %collective-permute-start.33 = (bf16[2,192,256]{2,1,0:T(8,128)(2,1)S(1)}, bf16[2,192,256]{2,1,0:T(8,128)(2,1)S(1)}, u32[]{:S(2)}, u32[]{:S(2)}) collective-permute-start(bf16[2,192,256]{2,1,0:T(8,128)(2,1)S(1)} %slice.47), channel_id=1, source_target_pairs={{0,8},{1,9},{2,10},{3,11},{4,12},{5,13},{6,14},{7,15},{8,0},{9,1},... | collective-permute-start | bytes 589832 | tf_op jit(solution)/shard_map/ppermute | solution.py:18
  70.4 9.8 %collective-permute-start.24 = (bf16[384,256]{1,0:T(8,128)(2,1)S(1)}, bf16[384,256]{1,0:T(8,128)(2,1)S(1)}, u32[]{:S(2)}, u32[]{:S(2)}) collective-permute-start(bf16[384,256]{1,0:T(8,128)(2,1)S(1)} %constant_dynamic-update-slice_fusion.refs_0_), channel_id=1, source_target_pairs={{0,12},{1,13},{2,14},{3,15},{4,8},{5,9},{6,10},{7,11},{8,4},{9,5},... | collective-permute-start | bytes 589832 | tf_op jit(solution)/shard_map/ppermute | solution.py:18
  71.9 12.5 %collective-permute-start.20 = (bf16[384,256]{1,0:T(8,128)(2,1)S(1)}, bf16[384,256]{1,0:T(8,128)(2,1)S(1)}, u32[]{:S(2)}, u32[]{:S(2)}) collective-permute-start(bf16[384,256]{1,0:T(8,128)(2,1)S(1)} %constant_dynamic-update-slice_fusion.refs_0_), channel_id=1, source_target_pairs={{0,4},{1,5},{2,6},{3,7},{4,0},{5,1},{6,2},{7,3},{8,12},{9,13},{10,... | collective-permute-start | bytes 589832 | tf_op jit(solution)/shard_map/ppermute | solution.py:18
  72.4 17.2 %collective-permute-start.22 = (bf16[384,256]{1,0:T(8,128)(2,1)S(1)}, bf16[384,256]{1,0:T(8,128)(2,1)S(1)}, u32[]{:S(2)}, u32[]{:S(2)}) collective-permute-start(bf16[384,256]{1,0:T(8,128)(2,1)S(1)} %constant_dynamic-update-slice_fusion.refs_0_), channel_id=1, source_target_pairs={{0,8},{1,9},{2,10},{3,11},{4,12},{5,13},{6,14},{7,15},{8,0},{9,1},... | collective-permute-start | bytes 589832 | tf_op jit(solution)/shard_map/ppermute | solution.py:18
  74.8 16.2 %collective-permute-start.19 = (bf16[384,256]{1,0:T(8,128)(2,1)S(1)}, bf16[384,256]{1,0:T(8,128)(2,1)S(1)}, u32[]{:S(2)}, u32[]{:S(2)}) collective-permute-start(bf16[384,256]{1,0:T(8,128)(2,1)S(1)} %constant_dynamic-update-slice_fusion.refs_0_), channel_id=1, source_target_pairs={{0,2},{1,3},{2,0},{3,1},{4,6},{5,7},{6,4},{7,5},{8,10},{9,11},{10,... | collective-permute-start | bytes 589832 | tf_op jit(solution)/shard_map/ppermute | solution.py:18
  77.1 14.0 %collective-permute-start.26 = (bf16[384,256]{1,0:T(8,128)(2,1)S(1)}, bf16[384,256]{1,0:T(8,128)(2,1)S(1)}, u32[]{:S(2)}, u32[]{:S(2)}) collective-permute-start(bf16[384,256]{1,0:T(8,128)(2,1)S(1)} %constant_dynamic-update-slice_fusion.refs_0_), channel_id=1, source_target_pairs={{0,1},{1,0},{2,3},{3,2},{4,5},{5,4},{6,7},{7,6},{8,9},{9,8},{10,11... | collective-permute-start | bytes 589832 | tf_op jit(solution)/shard_map/ppermute | solution.py:18
  87.1 12.9 %collective-permute-start.41 = (bf16[192,512]{1,0:T(8,128)(2,1)S(1)}, bf16[192,512]{1,0:T(8,128)(2,1)}, u32[]{:S(2)}, u32[]{:S(2)}) collective-permute-start(bf16[192,512]{1,0:T(8,128)(2,1)S(1)} %bitcast.21), channel_id=1, source_target_pairs={{0,16},{16,0},{1,17},{17,1},{2,18},{18,2},{3,19},{19,3},{4,20},{20... | collective-permute-start | bytes 589832 | tf_op jit(solution)/shard_map/ppermute | solution.py:18
  91.1 9.4 %collective-permute-start.28 = (bf16[384,256]{1,0:T(8,128)(2,1)S(1)}, bf16[384,256]{1,0:T(8,128)(2,1)S(1)}, u32[]{:S(2)}, u32[]{:S(2)}) collective-permute-start(bf16[384,256]{1,0:T(8,128)(2,1)S(1)} %collective-permute-done.20.refs_2_), channel_id=1, source_target_pairs={{0,1},{1,0},{2,3},{3,2},{4,5},{5,4},{6,7},{7,6},{8,9},{9,8},{10,11... | collective-permute-start | bytes 589832 | tf_op jit(solution)/shard_map/ppermute | solution.py:18
  91.1 8.8 %collective-permute-start.23 = (bf16[384,256]{1,0:T(8,128)(2,1)S(1)}, bf16[384,256]{1,0:T(8,128)(2,1)S(1)}, u32[]{:S(2)}, u32[]{:S(2)}) collective-permute-start(bf16[384,256]{1,0:T(8,128)(2,1)S(1)} %collective-permute-done.22.refs_4_), channel_id=1, source_target_pairs={{0,2},{1,3},{2,0},{3,1},{4,6},{5,7},{6,4},{7,5},{8,10},{9,11},{10,... | collective-permute-start | bytes 589832 | tf_op jit(solution)/shard_map/ppermute | solution.py:18
  91.6 8.8 %collective-permute-start.27 = (bf16[384,256]{1,0:T(8,128)(2,1)S(1)}, bf16[384,256]{1,0:T(8,128)(2,1)S(1)}, u32[]{:S(2)}, u32[]{:S(2)}) collective-permute-start(bf16[384,256]{1,0:T(8,128)(2,1)S(1)} %collective-permute-done.19.refs_1_), channel_id=1, source_target_pairs={{0,1},{1,0},{2,3},{3,2},{4,5},{5,4},{6,7},{7,6},{8,9},{9,8},{10,11... | collective-permute-start | bytes 589832 | tf_op jit(solution)/shard_map/ppermute | solution.py:18
  (37 other events, 255.1 us)

commit v3 on v2

--- a/solution.py
+++ b/solution.py
@@ -262,38 +262,6 @@
         compiler_params=pltpu.CompilerParams(dimension_semantics=("arbitrary",)),
         name="project",
     )(order, *sides, w_out, w_out, w_out, w_out, x)
-
-
-def out_whole_kernel(order, *refs, length, local):
-    count = len(RELATIVE)
-    pieces, weights, x, out = refs[:count], refs[count], refs[count + 1], refs[count + 2]
-    here, sems = refs[count + 3 :]
-    for copy in copies_in(weights, here, sems):
-        copy.wait()
-    total = x[:length, :].astype(F32)
-    for slot, piece in enumerate(pieces):
-        place = pl.ds(pl.multiple_of(order[slot] * local, local), local)
-        total = total + jnp.dot(piece[:length, :], here[place, :], preferred_element_type=F32)
-    out[...] = total.astype(BF16)
-
-
-def project_whole(order, pieces, w_out, x):
-    width = x.shape[1]
-    length = x.shape[0] - EXTRA
-    local = pieces[0].shape[1]
-    whole = pl.BlockSpec(memory_space=pltpu.VMEM)
-    return pl.pallas_call(
-        functools.partial(out_whole_kernel, length=length, local=local),
-        out_shape=jax.ShapeDtypeStruct((length, width), BF16),
-        in_specs=[pl.BlockSpec(memory_space=pltpu.SMEM)]
-        + [whole] * len(pieces)
-        + [pl.BlockSpec(memory_space=pltpu.HBM), whole],
-        out_specs=whole,
-        scratch_shapes=[pltpu.VMEM(w_out.shape, w_out.dtype), pltpu.SemaphoreType.DMA((8,))],
-        compiler_params=pltpu.CompilerParams(vmem_limit_bytes=16 * 2**20),
-        cost_estimate=FREE,
-        name="project",
-    )(order, *pieces, w_out, x)
 
 
 def eliminate(block):
@@ -439,12 +407,13 @@
     return (block_out, filter_grad, basis, right_factor)
 
 
-def finish_kernel(flag, *refs):
+def finish_kernel(flag, order, *refs):
     count = len(RELATIVE)
     pieces = refs[:count]
-    side_own, side_other, cot_own, cot_other = refs[count : count + 4]
-    basis, right_raw, sums = refs[count + 4 : count + 7]
-    rows, cots, sides, inverse = refs[count + 7 :]
+    side_own, side_other, cot_own, cot_other, x, weights = refs[count : count + 6]
+    block_out, basis, right_raw, sums = refs[count + 6 : count + 10]
+    rows, cots, sides, inverse, here, sems = refs[count + 10 :]
+    copies = copies_in(weights, here, sems)
     mine = flag[0]
     other = 1 - mine
     length = cots.shape[1]
@@ -470,6 +439,13 @@
     under = dot_high(across_t, turned[0], plain) + dot_high(end, turned[1], plain)
     rowwise = ((0,), (0,))
     gram = dot_high(turned[0], upper, rowwise) + dot_high(turned[1], under, rowwise)
+    for copy in copies:
+        copy.wait()
+    total = x[:length, :].astype(F32)
+    for slot, piece in enumerate(pieces):
+        place = pl.ds(pl.multiple_of(order[slot] * local, local), local)
+        total = total + jnp.dot(piece[:length, :], here[place, :], preferred_element_type=F32)
+    block_out[...] = total.astype(BF16)
     factor_kernel(gram, inverse)
     scaled = inverse[...] * math.sqrt(local * count)
     panel = jnp.zeros((local, gram.shape[0]), F32)
@@ -489,7 +465,7 @@
     sums[...] = jnp.sum(raw * raw, axis=0, keepdims=True)
 
 
-def finish(flag, pieces, side_own, side_other, cot_own, cot_other):
+def finish(flag, order, pieces, side_own, side_other, cot_own, cot_other, x, w_out):
     local = pieces[0].shape[1]
     length, width = cot_own.shape
     rank = side_own.shape[1]
@@ -498,22 +474,27 @@
     return pl.pallas_call(
         finish_kernel,
         out_shape=(
+            jax.ShapeDtypeStruct((length, width), BF16),
             jax.ShapeDtypeStruct((local, rank), BF16),
             jax.ShapeDtypeStruct((width, rank), F32),
             jax.ShapeDtypeStruct((1, rank), F32),
         ),
-        in_specs=[pl.BlockSpec(memory_space=pltpu.SMEM)] + [whole] * (count + 4),
-        out_specs=(whole, whole, whole),
+        in_specs=[pl.BlockSpec(memory_space=pltpu.SMEM)] * 2
+        + [whole] * (count + 5)
+        + [pl.BlockSpec(memory_space=pltpu.HBM)],
+        out_specs=(whole,) * 4,
         scratch_shapes=[
             pltpu.VMEM((2, length, count * local), BF16),
             pltpu.VMEM((2, length, width), BF16),
             pltpu.VMEM((2, length, rank), F32),
             pltpu.VMEM((rank, rank), F32),
+            pltpu.VMEM(w_out.shape, w_out.dtype),
+            pltpu.SemaphoreType.DMA((8,)),
         ],
         compiler_params=pltpu.CompilerParams(vmem_limit_bytes=20 * 2**20),
         cost_estimate=pl.CostEstimate(flops=2**33, transcendentals=0, bytes_accessed=2**22),
         name="finish",
-    )(flag, *pieces, side_own, side_other, cot_own, cot_other)
+    )(flag, order, *pieces, side_own, side_other, cot_own, cot_other, x, w_out)
 
 
 FREE = pl.CostEstimate(flops=1, transcendentals=0, bytes_accessed=1)
@@ -624,7 +605,7 @@
             pltpu.VMEM((length, width), BF16),
             pltpu.VMEM((length + 16, local), F32),
             pltpu.VMEM(w_in.shape, w_in.dtype),
-            pltpu.SemaphoreType.DMA((3, 4)),
+            pltpu.SemaphoreType.DMA((3, 1)),
         ],
         compiler_params=pltpu.CompilerParams(vmem_limit_bytes=24 * 2**20),
         cost_estimate=pl.CostEstimate(
@@ -704,14 +685,13 @@
     away, keep = grad_parts(targets, w_out, cot_cols, size)
     keep = keep.astype(F32) + send(away, bits=1).astype(F32)
     away, keep = keep[:4].astype(BF16), keep[4:]
-    keep = keep + send(away, bits=2).astype(F32)
-    away, keep = keep[:2].astype(BF16), keep[2:]
     side = jnp.dot(cot_cols, right_prev, preferred_element_type=F32)
     side = both_ways(side, 1, size)
     ready = after(order, side, away, keep)
     y, qkv, saved = mix_whole(ready, [have[r] for r in RELATIVE], w_in, feat, inner)
 
-    keep = keep + send(away, bits=8).astype(F32)
+    keep = keep + send(away, bits=2).astype(F32)
+    keep = keep[2:] + send(keep[:2].astype(BF16), bits=8).astype(F32)
     y_grad = (keep[1:] + send(keep[:1].astype(BF16), bits=4).astype(F32))[0]
     for bits in (2, 4, 8):
         side = both_ways(side, bits, size)
@@ -728,11 +708,12 @@
     filter_grad = jnp.swapaxes(filter_grad.reshape(4, 8, groups), 1, 2)[:, :, : inner.shape[0]]
     got[15] = send(after(got[14], terms), bits=1)
     pieces = [got[r] for r in RELATIVE]
-    basis, right_raw, sums = finish(flag, pieces, side, side_other, cot_cols, cot_other)
+    block_out, basis, right_raw, sums = finish(
+        flag, order, pieces, side, side_other, cot_cols, cot_other, x_sent, w_out
+    )
     column_sums = plane_sum(sums, size)
-    block_out = project_whole(order, pieces, w_out, x_sent)[None]
     right_factor = right_raw * lax.rsqrt(column_sums / (size * width) + 1e-06)
-    return (block_out, filter_grad, basis, right_factor)
+    return (block_out[None], filter_grad, basis, right_factor)
 
 
 def per_device(ids, embed, gain, w_in, feat_filter, inner_filter, w_out, cotangent, right_prev):

time: 135 us -> 130 us (0.963)
  waiting for transfers between devices: 40.9 us -> 47.5 us
  Pallas kernels: 38.5 us -> 33.6 us
  starting transfers between devices: 44.4 us -> 40 us
  local copies, waits for them, and re-layouts: 4.67 us -> 1.83 us
  matrix products: 0.52 us -> 2.3 us
    ppermute x46, waiting for transfers between devices: 40.9 us -> 47.5 us  [exchange(): return lax.ppermute(value, axis, [(i, i ^ bits) for i in range(size)])]
    pallas_call x2 -> x1, Pallas kernels: 20.7 us -> 16.2 us  [finish(): pl.pallas_call(finish_kernel, out_shape=(jax.ShapeDtypeStruct((length, wi...]
    ppermute x46, starting transfers between devices: 44.4 us -> 40 us  [exchange(): return lax.ppermute(value, axis, [(i, i ^ bits) for i in range(size)])]
    unnamed x31 -> x21, local copies, waits for them, and re-layouts: 3.58 us -> 0.06 us
  transfers between devices with their start and end apart: 46 -> 46, of which waited for: 18 -> 18; matrix products, arithmetic and copies ran while one was open for 3% -> 4% of each run, Pallas kernels for 14% -> 13%
where the time goes in v3:
time: 130 us
  waiting for transfers between devices  47.5 us (37%)
  starting transfers between devices  40 us (31%)
  Pallas kernels  33.6 us (26%)
  other arithmetic  3.86 us (3%)
  matrix products  2.3 us (2%)
  local copies, waits for them, and re-layouts  1.83 us (1%)
    ppermute x46, waiting for transfers between devices, exchange(): return lax.ppermute(value, axis, [(i, i ^ bits) for i in range(size)])  47.5 us
    ppermute x46, starting transfers between devices, exchange(): return lax.ppermute(value, axis, [(i, i ^ bits) for i in range(size)])  40 us
    pallas_call x1, Pallas kernels, finish(): pl.pallas_call(finish_kernel, out_shape=(jax.ShapeDtypeStruct((length, wi...  16.2 us
    pallas_call x1, Pallas kernels, mix_whole(): pl.pallas_call(functools.partial(mix_whole_kernel, length=length), out_sh...  9.76 us
    pallas_call x1, Pallas kernels, grad_parts(): pl.pallas_call(functools.partial(parts_kernel, local=local), out_shape=(s...  4.27 us
    pallas_call x1, Pallas kernels, filter_terms(): pl.pallas_call(functools.partial(terms_kernel, scale=scale), out_shape=ja...  3.34 us
  transfers between devices with their start and end apart: 46, of which 18 were waited for; matrix products, arithmetic and copies ran while one was open for 4% of the time, Pallas kernels for 13%

profile of v3, /device:TPU:0, one launch (start us, length us, event | category | flops | bytes accessed | tf_op | source)
XLA Modules:
  0.0 130.0 jit_solution(9618705797178854534)
XLA Ops:
  4.2 2.7 %collective-permute-start.3 = (bf16[208,512]{1,0:T(8,128)(2,1)S(1)}, bf16[208,512]{1,0:T(8,128)(2,1)S(1)}, u32[]{:S(2)}, u32[]{:S(2)}) collective-permute-start(bf16[208,512]{1,0:T(8,128)(2,1)S(1)} %pad_maximum_fusion.refs_0_.refs_20_), channel_id=1, source_target_pairs={{0,4},{1,5},{2,6},{3,7},{4,0},{5,1},{6,2},{7,3},{8,12},{9,13},{10,... | collective-permute-start | bytes 638984 | tf_op jit(solution)/shard_map/ppermute | solution.py:18
  6.9 2.6 %collective-permute-start.5 = (bf16[208,512]{1,0:T(8,128)(2,1)S(1)}, bf16[208,512]{1,0:T(8,128)(2,1)S(1)}, u32[]{:S(2)}, u32[]{:S(2)}) collective-permute-start(bf16[208,512]{1,0:T(8,128)(2,1)S(1)} %pad_maximum_fusion.refs_0_.refs_20_), channel_id=1, source_target_pairs={{0,8},{1,9},{2,10},{3,11},{4,12},{5,13},{6,14},{7,15},{8,0},{9,1},... | collective-permute-start | bytes 638984 | tf_op jit(solution)/shard_map/ppermute | solution.py:18
  9.5 1.8 %collective-permute-start.36 = (bf16[192,256]{1,0:T(8,128)(2,1)S(1)}, bf16[192,256]{1,0:T(8,128)(2,1)S(1)}, u32[]{:S(2)}, u32[]{:S(2)}) collective-permute-start(bf16[192,256]{1,0:T(8,128)(2,1)S(1)} %fusion.4), channel_id=1, source_target_pairs={{0,2},{1,3},{2,0},{3,1},{4,6},{5,7},{6,4},{7,5},{8,10},{9,11},{10,... | collective-permute-start | bytes 294920 | tf_op jit(solution)/shard_map/ppermute | solution.py:18
  11.3 4.3 %grad_parts.1 = (bf16[8,192,256]{2,1,0:T(8,128)(2,1)S(1)}, bf16[8,192,256]{2,1,0:T(8,128)(2,1)S(1)}) custom-call(s32[16]{0:T(128)S(1)} %broadcast_xor_fusion.order, bf16[4096,512]{1,0:T(8,128)(2,1)} %refs_21_.1, bf16[192,512]{1,0:T(8,128)(2,1)S(1)} %bitcast.20), custom_call_target="tpu_custom_call" | custom-call | flops 1 | bytes 1 | tf_op jit(solution)/shard_map/grad_parts/pallas_call | solution.py:531
  16.9 1.7 %collective-permute-start.2 = (bf16[208,512]{1,0:T(8,128)(2,1)S(1)}, bf16[208,512]{1,0:T(8,128)(2,1)S(1)}, u32[]{:S(2)}, u32[]{:S(2)}) collective-permute-start(bf16[208,512]{1,0:T(8,128)(2,1)S(1)} %pad_maximum_fusion.refs_0_.refs_20_), channel_id=1, source_target_pairs={{0,2},{1,3},{2,0},{3,1},{4,6},{5,7},{6,4},{7,5},{8,10},{9,11},{10,... | collective-permute-start | bytes 638984 | tf_op jit(solution)/shard_map/ppermute | solution.py:18
  18.6 6.5 %collective-permute-done.5.refs_4_ = bf16[208,512]{1,0:T(8,128)(2,1)S(1)} collective-permute-done((bf16[208,512]{1,0:T(8,128)(2,1)S(1)}, bf16[208,512]{1,0:T(8,128)(2,1)S(1)}, u32[]{:S(2)}, u32[]{:S(2)}) %collective-permute-start.5) | collective-permute-done | bytes 213024 | tf_op jit(solution)/shard_map/ppermute | solution.py:18
  26.6 3.9 %collective-permute-start.38 = (bf16[192,256]{1,0:T(8,128)(2,1)S(1)}, bf16[192,256]{1,0:T(8,128)(2,1)S(1)}, u32[]{:S(2)}, u32[]{:S(2)}) collective-permute-start(bf16[192,256]{1,0:T(8,128)(2,1)S(1)} %add_convert_fusion), channel_id=1, source_target_pairs={{0,8},{1,9},{2,10},{3,11},{4,12},{5,13},{6,14},{7,15},{8,0},{9,1},... | collective-permute-start | bytes 294920 | tf_op jit(solution)/shard_map/ppermute | solution.py:18
  32.1 2.9 %collective-permute-done.38 = bf16[192,256]{1,0:T(8,128)(2,1)S(1)} collective-permute-done((bf16[192,256]{1,0:T(8,128)(2,1)S(1)}, bf16[192,256]{1,0:T(8,128)(2,1)S(1)}, u32[]{:S(2)}, u32[]{:S(2)}) %collective-permute-start.38) | collective-permute-done | bytes 98336 | tf_op jit(solution)/shard_map/ppermute | solution.py:18
  38.4 4.3 %collective-permute-done.8.refs_7_ = bf16[208,512]{1,0:T(8,128)(2,1)S(1)} collective-permute-done((bf16[208,512]{1,0:T(8,128)(2,1)S(1)}, bf16[208,512]{1,0:T(8,128)(2,1)S(1)}, u32[]{:S(2)}, u32[]{:S(2)}) %collective-permute-start.8) | collective-permute-done | bytes 213024 | tf_op jit(solution)/shard_map/ppermute | solution.py:18
  44.9 1.6 %collective-permute-start.39 = (f32[192,256]{1,0:T(8,128)S(1)}, f32[192,256]{1,0:T(8,128)S(1)}, u32[]{:S(2)}, u32[]{:S(2)}) collective-permute-start(f32[192,256]{1,0:T(8,128)S(1)} %convert_add_fusion.2.refs_16_), channel_id=1, source_target_pairs={{0,16},{16,0},{1,17},{17,1},{2,18},{18,2},{3,19},{19,3},{4,20},{20... | collective-permute-start | bytes 589832 | tf_op jit(solution)/shard_map/ppermute | solution.py:18
  46.5 9.8 %mix.1 = (bf16[192,256]{1,0:T(8,128)(2,1)S(1)}, bf16[3,192,256]{2,1,0:T(8,128)(2,1)S(1)}, f32[5,192,256]{2,1,0:T(8,128)S(1)}) custom-call(s32[16]{0:T(128)S(1)} %broadcast_xor_fusion.1.order, bf16[208,512]{1,0:T(8,128)(2,1)S(1)} %pad_maximum_fusion.refs_0_.refs_20_, bf16[208,512]{1,0:T(8,128)(2,1)S(1)} %collective-permute-done.2.refs_1_, ...), custom_call_target="tpu_custom_call" | custom-call | flops 2415919104 | bytes 12582912 | tf_op jit(solution)/shard_map/mix/pallas_call | solution.py:593
  58.0 3.0 %collective-permute-done.17 = bf16[192,256]{1,0:T(8,128)(2,1)S(1)} collective-permute-done((bf16[192,256]{1,0:T(8,128)(2,1)S(1)}, bf16[192,256]{1,0:T(8,128)(2,1)S(1)}, u32[]{:S(2)}, u32[]{:S(2)}) %collective-permute-start.17) | collective-permute-done | bytes 98336 | tf_op jit(solution)/shard_map/ppermute | solution.py:18
  61.0 2.6 %collective-permute-start.23 = (bf16[384,256]{1,0:T(8,128)(2,1)S(1)}, bf16[384,256]{1,0:T(8,128)(2,1)S(1)}, u32[]{:S(2)}, u32[]{:S(2)}) collective-permute-start(bf16[384,256]{1,0:T(8,128)(2,1)S(1)} %constant_dynamic-update-slice_fusion.refs_0_), channel_id=1, source_target_pairs={{0,12},{1,13},{2,14},{3,15},{4,8},{5,9},{6,10},{7,11},{8,4},{9,5},... | collective-permute-start | bytes 589832 | tf_op jit(solution)/shard_map/ppermute | solution.py:18
  63.5 1.9 %collective-permute-start.21 = (bf16[384,256]{1,0:T(8,128)(2,1)S(1)}, bf16[384,256]{1,0:T(8,128)(2,1)S(1)}, u32[]{:S(2)}, u32[]{:S(2)}) collective-permute-start(bf16[384,256]{1,0:T(8,128)(2,1)S(1)} %constant_dynamic-update-slice_fusion.refs_0_), channel_id=1, source_target_pairs={{0,8},{1,9},{2,10},{3,11},{4,12},{5,13},{6,14},{7,15},{8,0},{9,1},... | collective-permute-start | bytes 589832 | tf_op jit(solution)/shard_map/ppermute | solution.py:18
  65.4 11.6 %collective-permute-done.33 = bf16[2,192,256]{2,1,0:T(8,128)(2,1)S(1)} collective-permute-done((bf16[2,192,256]{2,1,0:T(8,128)(2,1)S(1)}, bf16[2,192,256]{2,1,0:T(8,128)(2,1)S(1)}, u32[]{:S(2)}, u32[]{:S(2)}) %collective-permute-start.33) | collective-permute-done | bytes 196640 | tf_op jit(solution)/shard_map/ppermute | solution.py:18
  77.2 2.1 %collective-permute-start.24 = (bf16[384,256]{1,0:T(8,128)(2,1)S(1)}, bf16[384,256]{1,0:T(8,128)(2,1)S(1)}, u32[]{:S(2)}, u32[]{:S(2)}) collective-permute-start(bf16[384,256]{1,0:T(8,128)(2,1)S(1)} %collective-permute-done.23.refs_6_), channel_id=1, source_target_pairs={{0,2},{1,3},{2,0},{3,1},{4,6},{5,7},{6,4},{7,5},{8,10},{9,11},{10,... | collective-permute-start | bytes 589832 | tf_op jit(solution)/shard_map/ppermute | solution.py:18
  79.3 3.6 %collective-permute-start.34 = (bf16[1,192,256]{2,1,0:T(8,128)(2,1)S(1)}, bf16[1,192,256]{2,1,0:T(8,128)(2,1)S(1)}, u32[]{:S(2)}, u32[]{:S(2)}) collective-permute-start(bf16[1,192,256]{2,1,0:T(8,128)(2,1)S(1)} %slice.48), channel_id=1, source_target_pairs={{0,4},{1,5},{2,6},{3,7},{4,0},{5,1},{6,2},{7,3},{8,12},{9,13},{10,... | collective-permute-start | bytes 294920 | tf_op jit(solution)/shard_map/ppermute | solution.py:18
  83.7 1.8 %collective-permute-done.21.refs_4_ = bf16[384,256]{1,0:T(8,128)(2,1)S(1)} collective-permute-done((bf16[384,256]{1,0:T(8,128)(2,1)S(1)}, bf16[384,256]{1,0:T(8,128)(2,1)S(1)}, u32[]{:S(2)}, u32[]{:S(2)}) %collective-permute-start.21) | collective-permute-done | bytes 196640 | tf_op jit(solution)/shard_map/ppermute | solution.py:18
  89.9 3.3 %filter_terms.1 = bf16[32,16]{1,0:T(8,128)(2,1)} custom-call(f32[192,256]{1,0:T(8,128)} %fusion.summed, bf16[3,192,256]{2,1,0:T(8,128)(2,1)} %copy-done.3, f32[5,192,256]{2,1,0:T(8,128)} %copy-done.1, f32[7,256]{1,0:T(8,128)} %copy-done.4, f32[256,16]{1,0:T(8,128)} %fusion.2.pool), custom_call_target="tpu_custom_call" | custom-call | flops 1 | bytes 1 | tf_op jit(solution)/shard_map/filter_terms/pallas_call | solution.py:630
  94.7 3.0 %collective-permute-done.22.refs_5_ = bf16[384,256]{1,0:T(8,128)(2,1)} collective-permute-done((bf16[384,256]{1,0:T(8,128)(2,1)S(1)}, bf16[384,256]{1,0:T(8,128)(2,1)}, u32[]{:S(2)}, u32[]{:S(2)}) %collective-permute-start.22) | collective-permute-done | bytes 196640 | tf_op jit(solution)/shard_map/ppermute | solution.py:18
  100.1 16.2 %finish.1 = (bf16[192,512]{1,0:T(8,128)(2,1)}, bf16[256,256]{1,0:T(8,128)(2,1)}, f32[512,256]{1,0:T(8,128)S(1)}, f32[1,256]{1,0:T(1,128)S(1)}) custom-call(s32[1]{0:T(128)} %bitcast.flag, s32[16]{0:T(128)S(1)} %broadcast_xor_fusion.1.order, bf16[384,256]{1,0:T(8,128)(2,1)S(1)} %constant_dynamic-update-slice_fusion.refs_0_, ...), custom_call_target="tpu_custom_call" | custom-call | flops 8589934592 | bytes 4194304 | tf_op jit(solution)/shard_map/finish/pallas_call | solution.py:474
  117.9 3.2 %collective-permute-done.43 = f32[1,256]{1,0:T(1,128)S(1)} collective-permute-done((f32[1,256]{1,0:T(1,128)S(1)}, f32[1,256]{1,0:T(1,128)S(1)}, u32[]{:S(2)}, u32[]{:S(2)}) %collective-permute-start.43) | collective-permute-done | bytes 1056 | tf_op jit(solution)/shard_map/ppermute | solution.py:18
  121.9 2.8 %collective-permute-done.44 = f32[1,256]{1,0:T(1,128)S(1)} collective-permute-done((f32[1,256]{1,0:T(1,128)S(1)}, f32[1,256]{1,0:T(1,128)S(1)}, u32[]{:S(2)}, u32[]{:S(2)}) %collective-permute-start.44) | collective-permute-done | bytes 1056 | tf_op jit(solution)/shard_map/ppermute | solution.py:18
  125.8 3.3 %collective-permute-done.45 = f32[1,256]{1,0:T(1,128)S(1)} collective-permute-done((f32[1,256]{1,0:T(1,128)S(1)}, f32[1,256]{1,0:T(1,128)S(1)}, u32[]{:S(2)}, u32[]{:S(2)}) %collective-permute-start.45) | collective-permute-done | bytes 1056 | tf_op jit(solution)/shard_map/ppermute | solution.py:18
  (125 shorter events, 28.7 us)
Async XLA Ops:
  4.2 12.7 %collective-permute-start.3 = (bf16[208,512]{1,0:T(8,128)(2,1)S(1)}, bf16[208,512]{1,0:T(8,128)(2,1)S(1)}, u32[]{:S(2)}, u32[]{:S(2)}) collective-permute-start(bf16[208,512]{1,0:T(8,128)(2,1)S(1)} %pad_maximum_fusion.refs_0_.refs_20_), channel_id=1, source_target_pairs={{0,4},{1,5},{2,6},{3,7},{4,0},{5,1},{6,2},{7,3},{8,12},{9,13},{10,... | collective-permute-start | bytes 638984 | tf_op jit(solution)/shard_map/ppermute | solution.py:18
  6.9 18.2 %collective-permute-start.5 = (bf16[208,512]{1,0:T(8,128)(2,1)S(1)}, bf16[208,512]{1,0:T(8,128)(2,1)S(1)}, u32[]{:S(2)}, u32[]{:S(2)}) collective-permute-start(bf16[208,512]{1,0:T(8,128)(2,1)S(1)} %pad_maximum_fusion.refs_0_.refs_20_), channel_id=1, source_target_pairs={{0,8},{1,9},{2,10},{3,11},{4,12},{5,13},{6,14},{7,15},{8,0},{9,1},... | collective-permute-start | bytes 638984 | tf_op jit(solution)/shard_map/ppermute | solution.py:18
  9.5 17.1 %collective-permute-start.7 = (bf16[208,512]{1,0:T(8,128)(2,1)S(1)}, bf16[208,512]{1,0:T(8,128)(2,1)S(1)}, u32[]{:S(2)}, u32[]{:S(2)}) collective-permute-start(bf16[208,512]{1,0:T(8,128)(2,1)S(1)} %pad_maximum_fusion.refs_0_.refs_20_), channel_id=1, source_target_pairs={{0,12},{1,13},{2,14},{3,15},{4,8},{5,9},{6,10},{7,11},{8,4},{9,5},... | collective-permute-start | bytes 638984 | tf_op jit(solution)/shard_map/ppermute | solution.py:18
  15.6 20.9 %collective-permute-start.1 = (bf16[8,192,256]{2,1,0:T(8,128)(2,1)S(1)}, bf16[8,192,256]{2,1,0:T(8,128)(2,1)}, u32[]{:S(2)}, u32[]{:S(2)}) collective-permute-start(bf16[8,192,256]{2,1,0:T(8,128)(2,1)S(1)} %get-tuple-element.18), channel_id=1, source_target_pairs={{0,1},{1,0},{2,3},{3,2},{4,5},{5,4},{6,7},{7,6},{8,9},{9,8},{10,11... | collective-permute-start | bytes 2359304 | tf_op jit(solution)/shard_map/ppermute | solution.py:18
  15.7 10.2 %collective-permute-start.37 = (bf16[192,256]{1,0:T(8,128)(2,1)S(1)}, bf16[192,256]{1,0:T(8,128)(2,1)S(1)}, u32[]{:S(2)}, u32[]{:S(2)}) collective-permute-start(bf16[192,256]{1,0:T(8,128)(2,1)S(1)} %add_convert_fusion.1), channel_id=1, source_target_pairs={{0,4},{1,5},{2,6},{3,7},{4,0},{5,1},{6,2},{7,3},{8,12},{9,13},{10,... | collective-permute-start | bytes 294920 | tf_op jit(solution)/shard_map/ppermute | solution.py:18
  16.9 13.6 %collective-permute-start.2 = (bf16[208,512]{1,0:T(8,128)(2,1)S(1)}, bf16[208,512]{1,0:T(8,128)(2,1)S(1)}, u32[]{:S(2)}, u32[]{:S(2)}) collective-permute-start(bf16[208,512]{1,0:T(8,128)(2,1)S(1)} %pad_maximum_fusion.refs_0_.refs_20_), channel_id=1, source_target_pairs={{0,2},{1,3},{2,0},{3,1},{4,6},{5,7},{6,4},{7,5},{8,10},{9,11},{10,... | collective-permute-start | bytes 638984 | tf_op jit(solution)/shard_map/ppermute | solution.py:18
  26.0 9.0 %collective-permute-start.4 = (bf16[208,512]{1,0:T(8,128)(2,1)S(1)}, bf16[208,512]{1,0:T(8,128)(2,1)S(1)}, u32[]{:S(2)}, u32[]{:S(2)}) collective-permute-start(bf16[208,512]{1,0:T(8,128)(2,1)S(1)} %collective-permute-done.3.refs_2_), channel_id=1, source_target_pairs={{0,2},{1,3},{2,0},{3,1},{4,6},{5,7},{6,4},{7,5},{8,10},{9,11},{10,... | collective-permute-start | bytes 638984 | tf_op jit(solution)/shard_map/ppermute | solution.py:18
  26.6 8.3 %collective-permute-start.38 = (bf16[192,256]{1,0:T(8,128)(2,1)S(1)}, bf16[192,256]{1,0:T(8,128)(2,1)S(1)}, u32[]{:S(2)}, u32[]{:S(2)}) collective-permute-start(bf16[192,256]{1,0:T(8,128)(2,1)S(1)} %add_convert_fusion), channel_id=1, source_target_pairs={{0,8},{1,9},{2,10},{3,11},{4,12},{5,13},{6,14},{7,15},{8,0},{9,1},... | collective-permute-start | bytes 294920 | tf_op jit(solution)/shard_map/ppermute | solution.py:18
  30.5 12.3 %collective-permute-start.11 = (bf16[208,512]{1,0:T(8,128)(2,1)S(1)}, bf16[208,512]{1,0:T(8,128)(2,1)S(1)}, u32[]{:S(2)}, u32[]{:S(2)}) collective-permute-start(bf16[208,512]{1,0:T(8,128)(2,1)S(1)} %collective-permute-done.3.refs_2_), channel_id=1, source_target_pairs={{0,1},{1,0},{2,3},{3,2},{4,5},{5,4},{6,7},{7,6},{8,9},{9,8},{10,11... | collective-permute-start | bytes 638984 | tf_op jit(solution)/shard_map/ppermute | solution.py:18
  35.0 8.3 %collective-permute-start.13 = (bf16[208,512]{1,0:T(8,128)(2,1)S(1)}, bf16[208,512]{1,0:T(8,128)(2,1)S(1)}, u32[]{:S(2)}, u32[]{:S(2)}) collective-permute-start(bf16[208,512]{1,0:T(8,128)(2,1)S(1)} %collective-permute-done.5.refs_4_), channel_id=1, source_target_pairs={{0,1},{1,0},{2,3},{3,2},{4,5},{5,4},{6,7},{7,6},{8,9},{9,8},{10,11... | collective-permute-start | bytes 638984 | tf_op jit(solution)/shard_map/ppermute | solution.py:18
  43.3 13.5 %collective-permute-start.32 = (bf16[4,192,256]{2,1,0:T(8,128)(2,1)S(1)}, bf16[4,192,256]{2,1,0:T(8,128)(2,1)S(1)}, u32[]{:S(2)}, u32[]{:S(2)}) collective-permute-start(bf16[4,192,256]{2,1,0:T(8,128)(2,1)S(1)} %slice.46), channel_id=1, source_target_pairs={{0,2},{1,3},{2,0},{3,1},{4,6},{5,7},{6,4},{7,5},{8,10},{9,11},{10,... | collective-permute-start | bytes 1179656 | tf_op jit(solution)/shard_map/ppermute | solution.py:18
  44.9 32.3 %collective-permute-start.39 = (f32[192,256]{1,0:T(8,128)S(1)}, f32[192,256]{1,0:T(8,128)S(1)}, u32[]{:S(2)}, u32[]{:S(2)}) collective-permute-start(f32[192,256]{1,0:T(8,128)S(1)} %convert_add_fusion.2.refs_16_), channel_id=1, source_target_pairs={{0,16},{16,0},{1,17},{17,1},{2,18},{18,2},{3,19},{19,3},{4,20},{20... | collective-permute-start | bytes 589832 | tf_op jit(solution)/shard_map/ppermute | solution.py:18
  57.0 20.1 %collective-permute-start.33 = (bf16[2,192,256]{2,1,0:T(8,128)(2,1)S(1)}, bf16[2,192,256]{2,1,0:T(8,128)(2,1)S(1)}, u32[]{:S(2)}, u32[]{:S(2)}) collective-permute-start(bf16[2,192,256]{2,1,0:T(8,128)(2,1)S(1)} %slice.47), channel_id=1, source_target_pairs={{0,8},{1,9},{2,10},{3,11},{4,12},{5,13},{6,14},{7,15},{8,0},{9,1},... | collective-permute-start | bytes 589832 | tf_op jit(solution)/shard_map/ppermute | solution.py:18
  61.0 16.3 %collective-permute-start.23 = (bf16[384,256]{1,0:T(8,128)(2,1)S(1)}, bf16[384,256]{1,0:T(8,128)(2,1)S(1)}, u32[]{:S(2)}, u32[]{:S(2)}) collective-permute-start(bf16[384,256]{1,0:T(8,128)(2,1)S(1)} %constant_dynamic-update-slice_fusion.refs_0_), channel_id=1, source_target_pairs={{0,12},{1,13},{2,14},{3,15},{4,8},{5,9},{6,10},{7,11},{8,4},{9,5},... | collective-permute-start | bytes 589832 | tf_op jit(solution)/shard_map/ppermute | solution.py:18
  63.5 15.8 %collective-permute-start.19 = (bf16[384,256]{1,0:T(8,128)(2,1)S(1)}, bf16[384,256]{1,0:T(8,128)(2,1)S(1)}, u32[]{:S(2)}, u32[]{:S(2)}) collective-permute-start(bf16[384,256]{1,0:T(8,128)(2,1)S(1)} %constant_dynamic-update-slice_fusion.refs_0_), channel_id=1, source_target_pairs={{0,4},{1,5},{2,6},{3,7},{4,0},{5,1},{6,2},{7,3},{8,12},{9,13},{10,... | collective-permute-start | bytes 589832 | tf_op jit(solution)/shard_map/ppermute | solution.py:18
  63.5 22.0 %collective-permute-start.21 = (bf16[384,256]{1,0:T(8,128)(2,1)S(1)}, bf16[384,256]{1,0:T(8,128)(2,1)S(1)}, u32[]{:S(2)}, u32[]{:S(2)}) collective-permute-start(bf16[384,256]{1,0:T(8,128)(2,1)S(1)} %constant_dynamic-update-slice_fusion.refs_0_), channel_id=1, source_target_pairs={{0,8},{1,9},{2,10},{3,11},{4,12},{5,13},{6,14},{7,15},{8,0},{9,1},... | collective-permute-start | bytes 589832 | tf_op jit(solution)/shard_map/ppermute | solution.py:18
  77.1 9.9 %collective-permute-start.18 = (bf16[384,256]{1,0:T(8,128)(2,1)S(1)}, bf16[384,256]{1,0:T(8,128)(2,1)S(1)}, u32[]{:S(2)}, u32[]{:S(2)}) collective-permute-start(bf16[384,256]{1,0:T(8,128)(2,1)S(1)} %constant_dynamic-update-slice_fusion.refs_0_), channel_id=1, source_target_pairs={{0,2},{1,3},{2,0},{3,1},{4,6},{5,7},{6,4},{7,5},{8,10},{9,11},{10,... | collective-permute-start | bytes 589832 | tf_op jit(solution)/shard_map/ppermute | solution.py:18
  77.2 10.4 %collective-permute-start.25 = (bf16[384,256]{1,0:T(8,128)(2,1)S(1)}, bf16[384,256]{1,0:T(8,128)(2,1)S(1)}, u32[]{:S(2)}, u32[]{:S(2)}) collective-permute-start(bf16[384,256]{1,0:T(8,128)(2,1)S(1)} %constant_dynamic-update-slice_fusion.refs_0_), channel_id=1, source_target_pairs={{0,1},{1,0},{2,3},{3,2},{4,5},{5,4},{6,7},{7,6},{8,9},{9,8},{10,11... | collective-permute-start | bytes 589832 | tf_op jit(solution)/shard_map/ppermute | solution.py:18
  77.2 10.4 %collective-permute-start.24 = (bf16[384,256]{1,0:T(8,128)(2,1)S(1)}, bf16[384,256]{1,0:T(8,128)(2,1)S(1)}, u32[]{:S(2)}, u32[]{:S(2)}) collective-permute-start(bf16[384,256]{1,0:T(8,128)(2,1)S(1)} %collective-permute-done.23.refs_6_), channel_id=1, source_target_pairs={{0,2},{1,3},{2,0},{3,1},{4,6},{5,7},{6,4},{7,5},{8,10},{9,11},{10,... | collective-permute-start | bytes 589832 | tf_op jit(solution)/shard_map/ppermute | solution.py:18
  79.3 9.7 %collective-permute-start.34 = (bf16[1,192,256]{2,1,0:T(8,128)(2,1)S(1)}, bf16[1,192,256]{2,1,0:T(8,128)(2,1)S(1)}, u32[]{:S(2)}, u32[]{:S(2)}) collective-permute-start(bf16[1,192,256]{2,1,0:T(8,128)(2,1)S(1)} %slice.48), channel_id=1, source_target_pairs={{0,4},{1,5},{2,6},{3,7},{4,0},{5,1},{6,2},{7,3},{8,12},{9,13},{10,... | collective-permute-start | bytes 294920 | tf_op jit(solution)/shard_map/ppermute | solution.py:18
  85.5 12.2 %collective-permute-start.40 = (bf16[192,512]{1,0:T(8,128)(2,1)S(1)}, bf16[192,512]{1,0:T(8,128)(2,1)S(1)}, u32[]{:S(2)}, u32[]{:S(2)}) collective-permute-start(bf16[192,512]{1,0:T(8,128)(2,1)S(1)} %bitcast.21), channel_id=1, source_target_pairs={{0,16},{16,0},{1,17},{17,1},{2,18},{18,2},{3,19},{19,3},{4,20},{20... | collective-permute-start | bytes 589832 | tf_op jit(solution)/shard_map/ppermute | solution.py:18
  87.6 10.7 %collective-permute-start.27 = (bf16[384,256]{1,0:T(8,128)(2,1)S(1)}, bf16[384,256]{1,0:T(8,128)(2,1)S(1)}, u32[]{:S(2)}, u32[]{:S(2)}) collective-permute-start(bf16[384,256]{1,0:T(8,128)(2,1)S(1)} %collective-permute-done.19.refs_2_), channel_id=1, source_target_pairs={{0,1},{1,0},{2,3},{3,2},{4,5},{5,4},{6,7},{7,6},{8,9},{9,8},{10,11... | collective-permute-start | bytes 589832 | tf_op jit(solution)/shard_map/ppermute | solution.py:18
  87.6 10.1 %collective-permute-start.22 = (bf16[384,256]{1,0:T(8,128)(2,1)S(1)}, bf16[384,256]{1,0:T(8,128)(2,1)}, u32[]{:S(2)}, u32[]{:S(2)}) collective-permute-start(bf16[384,256]{1,0:T(8,128)(2,1)S(1)} %collective-permute-done.21.refs_4_), channel_id=1, source_target_pairs={{0,2},{1,3},{2,0},{3,1},{4,6},{5,7},{6,4},{7,5},{8,10},{9,11},{10,... | collective-permute-start | bytes 589832 | tf_op jit(solution)/shard_map/ppermute | solution.py:18
  89.0 9.2 %collective-permute-start.26 = (bf16[384,256]{1,0:T(8,128)(2,1)S(1)}, bf16[384,256]{1,0:T(8,128)(2,1)}, u32[]{:S(2)}, u32[]{:S(2)}) collective-permute-start(bf16[384,256]{1,0:T(8,128)(2,1)S(1)} %collective-permute-done.18.refs_1_), channel_id=1, source_target_pairs={{0,1},{1,0},{2,3},{3,2},{4,5},{5,4},{6,7},{7,6},{8,9},{9,8},{10,11... | collective-permute-start | bytes 589832 | tf_op jit(solution)/shard_map/ppermute | solution.py:18
  (32 other events, 230.6 us)

commit v4 on v3

--- a/solution.py
+++ b/solution.py
@@ -680,7 +680,7 @@
     w_out = pltpu.with_memory_space_constraint(w_out, pltpu.HBM)
 
     cot_cols = cotangent[0]
-    turns = [c + x + f + n for c in (1, 0) for x in (2, 0) for f in (8, 0) for n in (4, 0)]
+    turns = [c + x + f + n for c in (1, 0) for x in (2, 0) for n in (4, 0) for f in (8, 0)]
     targets = jnp.bitwise_xor(index, jnp.array(turns, jnp.int32))
     away, keep = grad_parts(targets, w_out, cot_cols, size)
     keep = keep.astype(F32) + send(away, bits=1).astype(F32)
@@ -691,8 +691,8 @@
     y, qkv, saved = mix_whole(ready, [have[r] for r in RELATIVE], w_in, feat, inner)
 
     keep = keep + send(away, bits=2).astype(F32)
-    keep = keep[2:] + send(keep[:2].astype(BF16), bits=8).astype(F32)
-    y_grad = (keep[1:] + send(keep[:1].astype(BF16), bits=4).astype(F32))[0]
+    keep = keep[2:] + send(keep[:2].astype(BF16), bits=4).astype(F32)
+    y_grad = (keep[1:] + send(keep[:1].astype(BF16), bits=8).astype(F32))[0]
     for bits in (2, 4, 8):
         side = both_ways(side, bits, size)
     side_other = exchange(side, "dp", count, 1)

time: 130 us -> 125 us (0.962)
  starting transfers between devices: 40 us -> 34.7 us
    ppermute x46, starting transfers between devices: 40 us -> 34.7 us  [exchange(): return lax.ppermute(value, axis, [(i, i ^ bits) for i in range(size)])]
  transfers between devices with their start and end apart: 46 -> 46, of which waited for: 18 -> 19; matrix products, arithmetic and copies ran while one was open for 4% -> 5% of each run, Pallas kernels for 13% -> 14%
where the time goes in v4:
time: 125 us
  waiting for transfers between devices  47.9 us (38%)
  starting transfers between devices  34.7 us (28%)
  Pallas kernels  33.6 us (27%)
  other arithmetic  3.86 us (3%)
  matrix products  2.3 us (2%)
  local copies, waits for them, and re-layouts  1.83 us (1%)
    ppermute x46, waiting for transfers between devices, exchange(): return lax.ppermute(value, axis, [(i, i ^ bits) for i in range(size)])  47.9 us
    ppermute x46, starting transfers between devices, exchange(): return lax.ppermute(value, axis, [(i, i ^ bits) for i in range(size)])  34.7 us
    pallas_call x1, Pallas kernels, finish(): pl.pallas_call(finish_kernel, out_shape=(jax.ShapeDtypeStruct((length, wi...  16.2 us
    pallas_call x1, Pallas kernels, mix_whole(): pl.pallas_call(functools.partial(mix_whole_kernel, length=length), out_sh...  9.76 us
    pallas_call x1, Pallas kernels, grad_parts(): pl.pallas_call(functools.partial(parts_kernel, local=local), out_shape=(s...  4.27 us
    pallas_call x1, Pallas kernels, filter_terms(): pl.pallas_call(functools.partial(terms_kernel, scale=scale), out_shape=ja...  3.34 us
  transfers between devices with their start and end apart: 46, of which 19 were waited for; matrix products, arithmetic and copies ran while one was open for 5% of the time, Pallas kernels for 14%

profile of v4, /device:TPU:0, one launch (start us, length us, event | category | flops | bytes accessed | tf_op | source)
XLA Modules:
  0.0 125.2 jit_solution(11256216442706123783)
XLA Ops:
  4.2 2.7 %collective-permute-start.3 = (bf16[208,512]{1,0:T(8,128)(2,1)S(1)}, bf16[208,512]{1,0:T(8,128)(2,1)S(1)}, u32[]{:S(2)}, u32[]{:S(2)}) collective-permute-start(bf16[208,512]{1,0:T(8,128)(2,1)S(1)} %pad_maximum_fusion.refs_0_.refs_20_), channel_id=1, source_target_pairs={{0,4},{1,5},{2,6},{3,7},{4,0},{5,1},{6,2},{7,3},{8,12},{9,13},{10,... | collective-permute-start | bytes 638984 | tf_op jit(solution)/shard_map/ppermute | solution.py:18
  6.9 2.6 %collective-permute-start.5 = (bf16[208,512]{1,0:T(8,128)(2,1)S(1)}, bf16[208,512]{1,0:T(8,128)(2,1)S(1)}, u32[]{:S(2)}, u32[]{:S(2)}) collective-permute-start(bf16[208,512]{1,0:T(8,128)(2,1)S(1)} %pad_maximum_fusion.refs_0_.refs_20_), channel_id=1, source_target_pairs={{0,8},{1,9},{2,10},{3,11},{4,12},{5,13},{6,14},{7,15},{8,0},{9,1},... | collective-permute-start | bytes 638984 | tf_op jit(solution)/shard_map/ppermute | solution.py:18
  9.5 1.8 %collective-permute-start.36 = (bf16[192,256]{1,0:T(8,128)(2,1)S(1)}, bf16[192,256]{1,0:T(8,128)(2,1)S(1)}, u32[]{:S(2)}, u32[]{:S(2)}) collective-permute-start(bf16[192,256]{1,0:T(8,128)(2,1)S(1)} %fusion.4), channel_id=1, source_target_pairs={{0,2},{1,3},{2,0},{3,1},{4,6},{5,7},{6,4},{7,5},{8,10},{9,11},{10,... | collective-permute-start | bytes 294920 | tf_op jit(solution)/shard_map/ppermute | solution.py:18
  11.3 4.3 %grad_parts.1 = (bf16[8,192,256]{2,1,0:T(8,128)(2,1)S(1)}, bf16[8,192,256]{2,1,0:T(8,128)(2,1)S(1)}) custom-call(s32[16]{0:T(128)S(1)} %broadcast_xor_fusion.order, bf16[4096,512]{1,0:T(8,128)(2,1)} %refs_21_.1, bf16[192,512]{1,0:T(8,128)(2,1)S(1)} %bitcast.20), custom_call_target="tpu_custom_call" | custom-call | flops 1 | bytes 1 | tf_op jit(solution)/shard_map/grad_parts/pallas_call | solution.py:531
  16.9 1.7 %collective-permute-start.2 = (bf16[208,512]{1,0:T(8,128)(2,1)S(1)}, bf16[208,512]{1,0:T(8,128)(2,1)S(1)}, u32[]{:S(2)}, u32[]{:S(2)}) collective-permute-start(bf16[208,512]{1,0:T(8,128)(2,1)S(1)} %pad_maximum_fusion.refs_0_.refs_20_), channel_id=1, source_target_pairs={{0,2},{1,3},{2,0},{3,1},{4,6},{5,7},{6,4},{7,5},{8,10},{9,11},{10,... | collective-permute-start | bytes 638984 | tf_op jit(solution)/shard_map/ppermute | solution.py:18
  18.6 6.5 %collective-permute-done.5.refs_4_ = bf16[208,512]{1,0:T(8,128)(2,1)S(1)} collective-permute-done((bf16[208,512]{1,0:T(8,128)(2,1)S(1)}, bf16[208,512]{1,0:T(8,128)(2,1)S(1)}, u32[]{:S(2)}, u32[]{:S(2)}) %collective-permute-start.5) | collective-permute-done | bytes 213024 | tf_op jit(solution)/shard_map/ppermute | solution.py:18
  26.6 3.9 %collective-permute-start.38 = (bf16[192,256]{1,0:T(8,128)(2,1)S(1)}, bf16[192,256]{1,0:T(8,128)(2,1)S(1)}, u32[]{:S(2)}, u32[]{:S(2)}) collective-permute-start(bf16[192,256]{1,0:T(8,128)(2,1)S(1)} %add_convert_fusion), channel_id=1, source_target_pairs={{0,8},{1,9},{2,10},{3,11},{4,12},{5,13},{6,14},{7,15},{8,0},{9,1},... | collective-permute-start | bytes 294920 | tf_op jit(solution)/shard_map/ppermute | solution.py:18
  32.1 2.9 %collective-permute-done.38 = bf16[192,256]{1,0:T(8,128)(2,1)S(1)} collective-permute-done((bf16[192,256]{1,0:T(8,128)(2,1)S(1)}, bf16[192,256]{1,0:T(8,128)(2,1)S(1)}, u32[]{:S(2)}, u32[]{:S(2)}) %collective-permute-start.38) | collective-permute-done | bytes 98336 | tf_op jit(solution)/shard_map/ppermute | solution.py:18
  38.4 4.3 %collective-permute-done.8.refs_7_ = bf16[208,512]{1,0:T(8,128)(2,1)S(1)} collective-permute-done((bf16[208,512]{1,0:T(8,128)(2,1)S(1)}, bf16[208,512]{1,0:T(8,128)(2,1)S(1)}, u32[]{:S(2)}, u32[]{:S(2)}) %collective-permute-start.8) | collective-permute-done | bytes 213024 | tf_op jit(solution)/shard_map/ppermute | solution.py:18
  44.9 1.6 %collective-permute-start.39 = (f32[192,256]{1,0:T(8,128)S(1)}, f32[192,256]{1,0:T(8,128)S(1)}, u32[]{:S(2)}, u32[]{:S(2)}) collective-permute-start(f32[192,256]{1,0:T(8,128)S(1)} %convert_add_fusion.2.refs_16_), channel_id=1, source_target_pairs={{0,16},{16,0},{1,17},{17,1},{2,18},{18,2},{3,19},{19,3},{4,20},{20... | collective-permute-start | bytes 589832 | tf_op jit(solution)/shard_map/ppermute | solution.py:18
  46.5 9.8 %mix.1 = (bf16[192,256]{1,0:T(8,128)(2,1)S(1)}, bf16[3,192,256]{2,1,0:T(8,128)(2,1)S(1)}, f32[5,192,256]{2,1,0:T(8,128)S(1)}) custom-call(s32[16]{0:T(128)S(1)} %broadcast_xor_fusion.1.order, bf16[208,512]{1,0:T(8,128)(2,1)S(1)} %pad_maximum_fusion.refs_0_.refs_20_, bf16[208,512]{1,0:T(8,128)(2,1)S(1)} %collective-permute-done.2.refs_1_, ...), custom_call_target="tpu_custom_call" | custom-call | flops 2415919104 | bytes 12582912 | tf_op jit(solution)/shard_map/mix/pallas_call | solution.py:593
  57.1 3.9 %collective-permute-done.17 = bf16[192,256]{1,0:T(8,128)(2,1)S(1)} collective-permute-done((bf16[192,256]{1,0:T(8,128)(2,1)S(1)}, bf16[192,256]{1,0:T(8,128)(2,1)S(1)}, u32[]{:S(2)}, u32[]{:S(2)}) %collective-permute-start.17) | collective-permute-done | bytes 98336 | tf_op jit(solution)/shard_map/ppermute | solution.py:18
  61.0 2.6 %collective-permute-start.23 = (bf16[384,256]{1,0:T(8,128)(2,1)S(1)}, bf16[384,256]{1,0:T(8,128)(2,1)S(1)}, u32[]{:S(2)}, u32[]{:S(2)}) collective-permute-start(bf16[384,256]{1,0:T(8,128)(2,1)S(1)} %constant_dynamic-update-slice_fusion.refs_0_), channel_id=1, source_target_pairs={{0,12},{1,13},{2,14},{3,15},{4,8},{5,9},{6,10},{7,11},{8,4},{9,5},... | collective-permute-start | bytes 589832 | tf_op jit(solution)/shard_map/ppermute | solution.py:18
  63.5 1.9 %collective-permute-start.21 = (bf16[384,256]{1,0:T(8,128)(2,1)S(1)}, bf16[384,256]{1,0:T(8,128)(2,1)S(1)}, u32[]{:S(2)}, u32[]{:S(2)}) collective-permute-start(bf16[384,256]{1,0:T(8,128)(2,1)S(1)} %constant_dynamic-update-slice_fusion.refs_0_), channel_id=1, source_target_pairs={{0,8},{1,9},{2,10},{3,11},{4,12},{5,13},{6,14},{7,15},{8,0},{9,1},... | collective-permute-start | bytes 589832 | tf_op jit(solution)/shard_map/ppermute | solution.py:18
  66.1 4.5 %collective-permute-done.23.refs_6_ = bf16[384,256]{1,0:T(8,128)(2,1)S(1)} collective-permute-done((bf16[384,256]{1,0:T(8,128)(2,1)S(1)}, bf16[384,256]{1,0:T(8,128)(2,1)S(1)}, u32[]{:S(2)}, u32[]{:S(2)}) %collective-permute-start.23) | collective-permute-done | bytes 196640 | tf_op jit(solution)/shard_map/ppermute | solution.py:18
  71.3 3.9 %collective-permute-done.19.refs_2_ = bf16[384,256]{1,0:T(8,128)(2,1)S(1)} collective-permute-done((bf16[384,256]{1,0:T(8,128)(2,1)S(1)}, bf16[384,256]{1,0:T(8,128)(2,1)S(1)}, u32[]{:S(2)}, u32[]{:S(2)}) %collective-permute-start.19) | collective-permute-done | bytes 196640 | tf_op jit(solution)/shard_map/ppermute | solution.py:18
  76.2 5.8 %collective-permute-done.21.refs_4_ = bf16[384,256]{1,0:T(8,128)(2,1)S(1)} collective-permute-done((bf16[384,256]{1,0:T(8,128)(2,1)S(1)}, bf16[384,256]{1,0:T(8,128)(2,1)S(1)}, u32[]{:S(2)}, u32[]{:S(2)}) %collective-permute-start.21) | collective-permute-done | bytes 196640 | tf_op jit(solution)/shard_map/ppermute | solution.py:18
  83.1 2.0 %collective-permute-start.22 = (bf16[384,256]{1,0:T(8,128)(2,1)S(1)}, bf16[384,256]{1,0:T(8,128)(2,1)}, u32[]{:S(2)}, u32[]{:S(2)}) collective-permute-start(bf16[384,256]{1,0:T(8,128)(2,1)S(1)} %collective-permute-done.21.refs_4_), channel_id=1, source_target_pairs={{0,2},{1,3},{2,0},{3,1},{4,6},{5,7},{6,4},{7,5},{8,10},{9,11},{10,... | collective-permute-start | bytes 589832 | tf_op jit(solution)/shard_map/ppermute | solution.py:18
  86.0 3.3 %filter_terms.1 = bf16[32,16]{1,0:T(8,128)(2,1)} custom-call(f32[192,256]{1,0:T(8,128)} %fusion.summed, bf16[3,192,256]{2,1,0:T(8,128)(2,1)} %copy-done.3, f32[5,192,256]{2,1,0:T(8,128)} %copy-done.1, f32[7,256]{1,0:T(8,128)} %copy-done.4, f32[256,16]{1,0:T(8,128)} %fusion.2.pool), custom_call_target="tpu_custom_call" | custom-call | flops 1 | bytes 1 | tf_op jit(solution)/shard_map/filter_terms/pallas_call | solution.py:630
  90.7 2.2 %collective-permute-done.22.refs_5_ = bf16[384,256]{1,0:T(8,128)(2,1)} collective-permute-done((bf16[384,256]{1,0:T(8,128)(2,1)S(1)}, bf16[384,256]{1,0:T(8,128)(2,1)}, u32[]{:S(2)}, u32[]{:S(2)}) %collective-permute-start.22) | collective-permute-done | bytes 196640 | tf_op jit(solution)/shard_map/ppermute | solution.py:18
  95.3 16.2 %finish.1 = (bf16[192,512]{1,0:T(8,128)(2,1)}, bf16[256,256]{1,0:T(8,128)(2,1)}, f32[512,256]{1,0:T(8,128)S(1)}, f32[1,256]{1,0:T(1,128)S(1)}) custom-call(s32[1]{0:T(128)} %bitcast.flag, s32[16]{0:T(128)S(1)} %broadcast_xor_fusion.1.order, bf16[384,256]{1,0:T(8,128)(2,1)S(1)} %constant_dynamic-update-slice_fusion.refs_0_, ...), custom_call_target="tpu_custom_call" | custom-call | flops 8589934592 | bytes 4194304 | tf_op jit(solution)/shard_map/finish/pallas_call | solution.py:474
  112.9 3.4 %collective-permute-done.43 = f32[1,256]{1,0:T(1,128)S(1)} collective-permute-done((f32[1,256]{1,0:T(1,128)S(1)}, f32[1,256]{1,0:T(1,128)S(1)}, u32[]{:S(2)}, u32[]{:S(2)}) %collective-permute-start.43) | collective-permute-done | bytes 1056 | tf_op jit(solution)/shard_map/ppermute | solution.py:18
  117.5 2.3 %collective-permute-done.44 = f32[1,256]{1,0:T(1,128)S(1)} collective-permute-done((f32[1,256]{1,0:T(1,128)S(1)}, f32[1,256]{1,0:T(1,128)S(1)}, u32[]{:S(2)}, u32[]{:S(2)}) %collective-permute-start.44) | collective-permute-done | bytes 1056 | tf_op jit(solution)/shard_map/ppermute | solution.py:18
  121.0 3.3 %collective-permute-done.45 = f32[1,256]{1,0:T(1,128)S(1)} collective-permute-done((f32[1,256]{1,0:T(1,128)S(1)}, f32[1,256]{1,0:T(1,128)S(1)}, u32[]{:S(2)}, u32[]{:S(2)}) %collective-permute-start.45) | collective-permute-done | bytes 1056 | tf_op jit(solution)/shard_map/ppermute | solution.py:18
  (125 shorter events, 26.8 us)
Async XLA Ops:
  4.2 12.7 %collective-permute-start.3 = (bf16[208,512]{1,0:T(8,128)(2,1)S(1)}, bf16[208,512]{1,0:T(8,128)(2,1)S(1)}, u32[]{:S(2)}, u32[]{:S(2)}) collective-permute-start(bf16[208,512]{1,0:T(8,128)(2,1)S(1)} %pad_maximum_fusion.refs_0_.refs_20_), channel_id=1, source_target_pairs={{0,4},{1,5},{2,6},{3,7},{4,0},{5,1},{6,2},{7,3},{8,12},{9,13},{10,... | collective-permute-start | bytes 638984 | tf_op jit(solution)/shard_map/ppermute | solution.py:18
  6.9 18.2 %collective-permute-start.5 = (bf16[208,512]{1,0:T(8,128)(2,1)S(1)}, bf16[208,512]{1,0:T(8,128)(2,1)S(1)}, u32[]{:S(2)}, u32[]{:S(2)}) collective-permute-start(bf16[208,512]{1,0:T(8,128)(2,1)S(1)} %pad_maximum_fusion.refs_0_.refs_20_), channel_id=1, source_target_pairs={{0,8},{1,9},{2,10},{3,11},{4,12},{5,13},{6,14},{7,15},{8,0},{9,1},... | collective-permute-start | bytes 638984 | tf_op jit(solution)/shard_map/ppermute | solution.py:18
  9.5 17.1 %collective-permute-start.7 = (bf16[208,512]{1,0:T(8,128)(2,1)S(1)}, bf16[208,512]{1,0:T(8,128)(2,1)S(1)}, u32[]{:S(2)}, u32[]{:S(2)}) collective-permute-start(bf16[208,512]{1,0:T(8,128)(2,1)S(1)} %pad_maximum_fusion.refs_0_.refs_20_), channel_id=1, source_target_pairs={{0,12},{1,13},{2,14},{3,15},{4,8},{5,9},{6,10},{7,11},{8,4},{9,5},... | collective-permute-start | bytes 638984 | tf_op jit(solution)/shard_map/ppermute | solution.py:18
  15.6 20.9 %collective-permute-start.1 = (bf16[8,192,256]{2,1,0:T(8,128)(2,1)S(1)}, bf16[8,192,256]{2,1,0:T(8,128)(2,1)}, u32[]{:S(2)}, u32[]{:S(2)}) collective-permute-start(bf16[8,192,256]{2,1,0:T(8,128)(2,1)S(1)} %get-tuple-element.18), channel_id=1, source_target_pairs={{0,1},{1,0},{2,3},{3,2},{4,5},{5,4},{6,7},{7,6},{8,9},{9,8},{10,11... | collective-permute-start | bytes 2359304 | tf_op jit(solution)/shard_map/ppermute | solution.py:18
  15.7 10.2 %collective-permute-start.37 = (bf16[192,256]{1,0:T(8,128)(2,1)S(1)}, bf16[192,256]{1,0:T(8,128)(2,1)S(1)}, u32[]{:S(2)}, u32[]{:S(2)}) collective-permute-start(bf16[192,256]{1,0:T(8,128)(2,1)S(1)} %add_convert_fusion.1), channel_id=1, source_target_pairs={{0,4},{1,5},{2,6},{3,7},{4,0},{5,1},{6,2},{7,3},{8,12},{9,13},{10,... | collective-permute-start | bytes 294920 | tf_op jit(solution)/shard_map/ppermute | solution.py:18
  16.9 13.6 %collective-permute-start.2 = (bf16[208,512]{1,0:T(8,128)(2,1)S(1)}, bf16[208,512]{1,0:T(8,128)(2,1)S(1)}, u32[]{:S(2)}, u32[]{:S(2)}) collective-permute-start(bf16[208,512]{1,0:T(8,128)(2,1)S(1)} %pad_maximum_fusion.refs_0_.refs_20_), channel_id=1, source_target_pairs={{0,2},{1,3},{2,0},{3,1},{4,6},{5,7},{6,4},{7,5},{8,10},{9,11},{10,... | collective-permute-start | bytes 638984 | tf_op jit(solution)/shard_map/ppermute | solution.py:18
  26.0 9.0 %collective-permute-start.4 = (bf16[208,512]{1,0:T(8,128)(2,1)S(1)}, bf16[208,512]{1,0:T(8,128)(2,1)S(1)}, u32[]{:S(2)}, u32[]{:S(2)}) collective-permute-start(bf16[208,512]{1,0:T(8,128)(2,1)S(1)} %collective-permute-done.3.refs_2_), channel_id=1, source_target_pairs={{0,2},{1,3},{2,0},{3,1},{4,6},{5,7},{6,4},{7,5},{8,10},{9,11},{10,... | collective-permute-start | bytes 638984 | tf_op jit(solution)/shard_map/ppermute | solution.py:18
  26.6 8.3 %collective-permute-start.38 = (bf16[192,256]{1,0:T(8,128)(2,1)S(1)}, bf16[192,256]{1,0:T(8,128)(2,1)S(1)}, u32[]{:S(2)}, u32[]{:S(2)}) collective-permute-start(bf16[192,256]{1,0:T(8,128)(2,1)S(1)} %add_convert_fusion), channel_id=1, source_target_pairs={{0,8},{1,9},{2,10},{3,11},{4,12},{5,13},{6,14},{7,15},{8,0},{9,1},... | collective-permute-start | bytes 294920 | tf_op jit(solution)/shard_map/ppermute | solution.py:18
  30.5 12.3 %collective-permute-start.11 = (bf16[208,512]{1,0:T(8,128)(2,1)S(1)}, bf16[208,512]{1,0:T(8,128)(2,1)S(1)}, u32[]{:S(2)}, u32[]{:S(2)}) collective-permute-start(bf16[208,512]{1,0:T(8,128)(2,1)S(1)} %collective-permute-done.3.refs_2_), channel_id=1, source_target_pairs={{0,1},{1,0},{2,3},{3,2},{4,5},{5,4},{6,7},{7,6},{8,9},{9,8},{10,11... | collective-permute-start | bytes 638984 | tf_op jit(solution)/shard_map/ppermute | solution.py:18
  35.0 8.3 %collective-permute-start.13 = (bf16[208,512]{1,0:T(8,128)(2,1)S(1)}, bf16[208,512]{1,0:T(8,128)(2,1)S(1)}, u32[]{:S(2)}, u32[]{:S(2)}) collective-permute-start(bf16[208,512]{1,0:T(8,128)(2,1)S(1)} %collective-permute-done.5.refs_4_), channel_id=1, source_target_pairs={{0,1},{1,0},{2,3},{3,2},{4,5},{5,4},{6,7},{7,6},{8,9},{9,8},{10,11... | collective-permute-start | bytes 638984 | tf_op jit(solution)/shard_map/ppermute | solution.py:18
  43.3 13.5 %collective-permute-start.32 = (bf16[4,192,256]{2,1,0:T(8,128)(2,1)S(1)}, bf16[4,192,256]{2,1,0:T(8,128)(2,1)S(1)}, u32[]{:S(2)}, u32[]{:S(2)}) collective-permute-start(bf16[4,192,256]{2,1,0:T(8,128)(2,1)S(1)} %slice.46), channel_id=1, source_target_pairs={{0,2},{1,3},{2,0},{3,1},{4,6},{5,7},{6,4},{7,5},{8,10},{9,11},{10,... | collective-permute-start | bytes 1179656 | tf_op jit(solution)/shard_map/ppermute | solution.py:18
  44.9 21.2 %collective-permute-start.39 = (f32[192,256]{1,0:T(8,128)S(1)}, f32[192,256]{1,0:T(8,128)S(1)}, u32[]{:S(2)}, u32[]{:S(2)}) collective-permute-start(f32[192,256]{1,0:T(8,128)S(1)} %convert_add_fusion.2.refs_16_), channel_id=1, source_target_pairs={{0,16},{16,0},{1,17},{17,1},{2,18},{18,2},{3,19},{19,3},{4,20},{20... | collective-permute-start | bytes 589832 | tf_op jit(solution)/shard_map/ppermute | solution.py:18
  57.0 8.5 %collective-permute-start.33 = (bf16[2,192,256]{2,1,0:T(8,128)(2,1)S(1)}, bf16[2,192,256]{2,1,0:T(8,128)(2,1)S(1)}, u32[]{:S(2)}, u32[]{:S(2)}) collective-permute-start(bf16[2,192,256]{2,1,0:T(8,128)(2,1)S(1)} %slice.47), channel_id=1, source_target_pairs={{0,4},{1,5},{2,6},{3,7},{4,0},{5,1},{6,2},{7,3},{8,12},{9,13},{10,... | collective-permute-start | bytes 589832 | tf_op jit(solution)/shard_map/ppermute | solution.py:18
  61.0 9.7 %collective-permute-start.23 = (bf16[384,256]{1,0:T(8,128)(2,1)S(1)}, bf16[384,256]{1,0:T(8,128)(2,1)S(1)}, u32[]{:S(2)}, u32[]{:S(2)}) collective-permute-start(bf16[384,256]{1,0:T(8,128)(2,1)S(1)} %constant_dynamic-update-slice_fusion.refs_0_), channel_id=1, source_target_pairs={{0,12},{1,13},{2,14},{3,15},{4,8},{5,9},{6,10},{7,11},{8,4},{9,5},... | collective-permute-start | bytes 589832 | tf_op jit(solution)/shard_map/ppermute | solution.py:18
  63.5 11.6 %collective-permute-start.19 = (bf16[384,256]{1,0:T(8,128)(2,1)S(1)}, bf16[384,256]{1,0:T(8,128)(2,1)S(1)}, u32[]{:S(2)}, u32[]{:S(2)}) collective-permute-start(bf16[384,256]{1,0:T(8,128)(2,1)S(1)} %constant_dynamic-update-slice_fusion.refs_0_), channel_id=1, source_target_pairs={{0,4},{1,5},{2,6},{3,7},{4,0},{5,1},{6,2},{7,3},{8,12},{9,13},{10,... | collective-permute-start | bytes 589832 | tf_op jit(solution)/shard_map/ppermute | solution.py:18
  63.5 18.5 %collective-permute-start.21 = (bf16[384,256]{1,0:T(8,128)(2,1)S(1)}, bf16[384,256]{1,0:T(8,128)(2,1)S(1)}, u32[]{:S(2)}, u32[]{:S(2)}) collective-permute-start(bf16[384,256]{1,0:T(8,128)(2,1)S(1)} %constant_dynamic-update-slice_fusion.refs_0_), channel_id=1, source_target_pairs={{0,8},{1,9},{2,10},{3,11},{4,12},{5,13},{6,14},{7,15},{8,0},{9,1},... | collective-permute-start | bytes 589832 | tf_op jit(solution)/shard_map/ppermute | solution.py:18
  65.4 17.6 %collective-permute-start.18 = (bf16[384,256]{1,0:T(8,128)(2,1)S(1)}, bf16[384,256]{1,0:T(8,128)(2,1)S(1)}, u32[]{:S(2)}, u32[]{:S(2)}) collective-permute-start(bf16[384,256]{1,0:T(8,128)(2,1)S(1)} %constant_dynamic-update-slice_fusion.refs_0_), channel_id=1, source_target_pairs={{0,2},{1,3},{2,0},{3,1},{4,6},{5,7},{6,4},{7,5},{8,10},{9,11},{10,... | collective-permute-start | bytes 589832 | tf_op jit(solution)/shard_map/ppermute | solution.py:18
  66.1 17.0 %collective-permute-start.25 = (bf16[384,256]{1,0:T(8,128)(2,1)S(1)}, bf16[384,256]{1,0:T(8,128)(2,1)S(1)}, u32[]{:S(2)}, u32[]{:S(2)}) collective-permute-start(bf16[384,256]{1,0:T(8,128)(2,1)S(1)} %constant_dynamic-update-slice_fusion.refs_0_), channel_id=1, source_target_pairs={{0,1},{1,0},{2,3},{3,2},{4,5},{5,4},{6,7},{7,6},{8,9},{9,8},{10,11... | collective-permute-start | bytes 589832 | tf_op jit(solution)/shard_map/ppermute | solution.py:18
  70.7 12.5 %collective-permute-start.24 = (bf16[384,256]{1,0:T(8,128)(2,1)S(1)}, bf16[384,256]{1,0:T(8,128)(2,1)S(1)}, u32[]{:S(2)}, u32[]{:S(2)}) collective-permute-start(bf16[384,256]{1,0:T(8,128)(2,1)S(1)} %collective-permute-done.23.refs_6_), channel_id=1, source_target_pairs={{0,2},{1,3},{2,0},{3,1},{4,6},{5,7},{6,4},{7,5},{8,10},{9,11},{10,... | collective-permute-start | bytes 589832 | tf_op jit(solution)/shard_map/ppermute | solution.py:18
  75.1 10.0 %collective-permute-start.34 = (bf16[1,192,256]{2,1,0:T(8,128)(2,1)S(1)}, bf16[1,192,256]{2,1,0:T(8,128)(2,1)S(1)}, u32[]{:S(2)}, u32[]{:S(2)}) collective-permute-start(bf16[1,192,256]{2,1,0:T(8,128)(2,1)S(1)} %slice.48), channel_id=1, source_target_pairs={{0,8},{1,9},{2,10},{3,11},{4,12},{5,13},{6,14},{7,15},{8,0},{9,1},... | collective-permute-start | bytes 294920 | tf_op jit(solution)/shard_map/ppermute | solution.py:18
  82.0 10.9 %collective-permute-start.40 = (bf16[192,512]{1,0:T(8,128)(2,1)S(1)}, bf16[192,512]{1,0:T(8,128)(2,1)S(1)}, u32[]{:S(2)}, u32[]{:S(2)}) collective-permute-start(bf16[192,512]{1,0:T(8,128)(2,1)S(1)} %bitcast.21), channel_id=1, source_target_pairs={{0,16},{16,0},{1,17},{17,1},{2,18},{18,2},{3,19},{19,3},{4,20},{20... | collective-permute-start | bytes 589832 | tf_op jit(solution)/shard_map/ppermute | solution.py:18
  83.1 10.4 %collective-permute-start.27 = (bf16[384,256]{1,0:T(8,128)(2,1)S(1)}, bf16[384,256]{1,0:T(8,128)(2,1)S(1)}, u32[]{:S(2)}, u32[]{:S(2)}) collective-permute-start(bf16[384,256]{1,0:T(8,128)(2,1)S(1)} %collective-permute-done.19.refs_2_), channel_id=1, source_target_pairs={{0,1},{1,0},{2,3},{3,2},{4,5},{5,4},{6,7},{7,6},{8,9},{9,8},{10,11... | collective-permute-start | bytes 589832 | tf_op jit(solution)/shard_map/ppermute | solution.py:18
  83.1 9.7 %collective-permute-start.22 = (bf16[384,256]{1,0:T(8,128)(2,1)S(1)}, bf16[384,256]{1,0:T(8,128)(2,1)}, u32[]{:S(2)}, u32[]{:S(2)}) collective-permute-start(bf16[384,256]{1,0:T(8,128)(2,1)S(1)} %collective-permute-done.21.refs_4_), channel_id=1, source_target_pairs={{0,2},{1,3},{2,0},{3,1},{4,6},{5,7},{6,4},{7,5},{8,10},{9,11},{10,... | collective-permute-start | bytes 589832 | tf_op jit(solution)/shard_map/ppermute | solution.py:18
  85.2 8.2 %collective-permute-start.26 = (bf16[384,256]{1,0:T(8,128)(2,1)S(1)}, bf16[384,256]{1,0:T(8,128)(2,1)}, u32[]{:S(2)}, u32[]{:S(2)}) collective-permute-start(bf16[384,256]{1,0:T(8,128)(2,1)S(1)} %collective-permute-done.18.refs_1_), channel_id=1, source_target_pairs={{0,1},{1,0},{2,3},{3,2},{4,5},{5,4},{6,7},{7,6},{8,9},{9,8},{10,11... | collective-permute-start | bytes 589832 | tf_op jit(solution)/shard_map/ppermute | solution.py:18
  (32 other events, 207.4 us)
